TPU v7x, 256 devices: a whole 4x4x8 slice. The times are simulated.
256 devices in a mesh: pairs: 64 (over z, y, core), cols: 4 (over x).
Axes of the slice: x: 4, y: 4, z: 8, core: 2. Of those that a mesh axis runs over, the one named last changes fastest.
Arguments:
- state: float32 [2, 64, 64, 16384], P(None, 'pairs', None, 'cols'), may hold values from -6 to 6
- sector_mix: float32 [127, 64, 64], P(None, None, 'cols'), may hold values from -2 to 2
- kerr_rates: float32 [2], replicated, may hold values from 0.002 to 0.02
- column_load: int32 [16384], P('cols'), may hold values from 0 to 255
Outputs:
- evolved: float32 [2, 64, 64, 16384], P(None, 'pairs', None, 'cols')
- moment: float32 [1], replicated
All inputs are finite; a program needn't handle non-finite values.
Results may differ from a plain program's by a relative error of at most 0.0003.
Values sent between devices are 32-bit elements; how exact they have to be, the bound alone decides.
No kernel may reach another device: no remote copies, remote signals or barrier semaphores. Data moves between devices by JAX's collectives and lax.ppermute only.
A program may use at most 128 MiB of HBM per device.

v0:
```python
import jax
import jax.numpy as jnp
import numpy as np
from jax import lax
from jax.sharding import PartitionSpec as P

THIRD = 64
MEMB = 128
WINDOW = 2


def build_tables(levels, pair_count):
    members = [[g] for g in range(2 * levels)]
    per_device = len(members) // pair_count
    per_source = levels // pair_count
    row_count = per_source * levels
    layout_rows = per_device * levels
    mat_index = -np.ones((pair_count, per_device, levels, levels), np.int64)
    buckets = [[[] for owner_id in range(pair_count)] for source_id in range(pair_count)]
    for group_id in range(len(members)):
        owner = group_id // per_device
        local_group = group_id % per_device
        offset = 0
        for sector in members[group_id]:
            if sector > 2 * levels - 2:
                continue
            low_end = max(0, sector - levels + 1)
            high_end = min(sector, levels - 1)
            sector_size = high_end - low_end + 1
            span = np.arange(sector_size)
            mat_index[
                owner, local_group, offset : offset + sector_size, offset : offset + sector_size
            ] = (sector * levels * levels + span[:, None] * levels + span[None, :])
            for step in range(sector_size):
                photon_one = low_end + step
                photon_two = sector - photon_one
                source = photon_one // per_source
                local_row = (photon_one - source * per_source) * levels + photon_two
                position = local_group * levels + offset + step
                buckets[source][owner].append((position, local_row))
            offset += sector_size
    slot_count = max((len(entries) for bucket_row in buckets for entries in bucket_row))
    send_idx = np.zeros((pair_count, pair_count, slot_count), np.int32)
    layout_idx = np.zeros((pair_count, layout_rows), np.int32)
    back_idx = np.zeros((pair_count, pair_count, slot_count), np.int32)
    row_idx = np.zeros((pair_count, row_count), np.int32)
    for source in range(pair_count):
        for owner in range(pair_count):
            entries = sorted(buckets[source][owner])
            for slot, (position, local_row) in enumerate(entries):
                send_idx[source, owner, slot] = local_row
                layout_idx[owner, position] = source * slot_count + slot
                back_idx[owner, source, slot] = position
                row_idx[source, local_row] = owner * slot_count + slot
    return (send_idx, layout_idx, back_idx, row_idx, mat_index.astype(np.int32), slot_count)


def local(state, sector_mix, kerr_rates, column_load):
    full_mix = lax.all_gather(sector_mix, "cols", axis=2, tiled=True)
    pair_count = lax.axis_size("pairs")
    device = lax.axis_index("pairs")
    col_device = lax.axis_index("cols")
    local_one = state.shape[1]
    levels = state.shape[2]
    col_count = state.shape[3]
    row_count = local_one * levels
    tables = build_tables(levels, pair_count)
    send_idx, layout_idx, back_idx, row_idx, mat_index, slot_count = tables
    flat_state = state.reshape(2, row_count, col_count)
    send_rows = jnp.asarray(send_idx)[device].reshape(-1)
    outgoing = jnp.take(flat_state, send_rows, axis=1).reshape(2, pair_count, slot_count, col_count)
    my_layout = jnp.asarray(layout_idx)[device]
    my_back = jnp.asarray(back_idx)[device].reshape(-1)
    my_mat = jnp.asarray(mat_index)[device]
    flat_mix = full_mix.reshape(-1)
    blocks = jnp.where(
        my_mat >= 0, jnp.take(flat_mix, jnp.maximum(my_mat, 0)), jnp.zeros((), jnp.float32)
    )
    groups = my_mat.shape[0]
    arrived = lax.all_to_all(outgoing, "pairs", split_axis=1, concat_axis=1, tiled=True)
    item_count = arrived.shape[3]
    gathered = jnp.take(arrived.reshape(2, pair_count * slot_count, item_count), my_layout, axis=1)
    gathered = gathered.reshape(2, groups, levels, item_count)
    combined = jnp.einsum("gij,pgjc->pgic", blocks, gathered, precision=lax.Precision.HIGHEST)
    leaving = jnp.take(combined.reshape(2, groups * levels, item_count), my_back, axis=1)
    leaving = leaving.reshape(2, pair_count, slot_count, item_count)
    returned = lax.all_to_all(leaving, "pairs", split_axis=1, concat_axis=1, tiled=True)
    mixed_rows = jnp.take(
        returned.reshape(2, pair_count * slot_count, col_count),
        jnp.asarray(row_idx)[device],
        axis=1,
    )
    real_part = mixed_rows[0]
    imag_part = mixed_rows[1]
    row_ids = jnp.arange(row_count, dtype=jnp.int32)
    photon_one = (device * local_one + row_ids // levels).astype(jnp.float32)
    photon_two = (row_ids % levels).astype(jnp.float32)
    loads = column_load.astype(jnp.float32)
    phases = (kerr_rates[0] * photon_one + kerr_rates[1] * photon_two)[:, None] * loads[None, :]
    cosine = jnp.cos(phases)
    sine_part = jnp.sin(phases)
    evolved = jnp.stack(
        [cosine * real_part - sine_part * imag_part, sine_part * real_part + cosine * imag_part]
    )
    evolved = evolved.reshape(2, local_one, levels, col_count)
    col_ids = col_device * col_count + jnp.arange(col_count, dtype=jnp.int32)
    third_level = (col_ids // (MEMB * WINDOW)).astype(jnp.float32)
    weight = (photon_one + 1.0)[:, None] * (third_level + 1.0)[None, :]
    partial_term = jnp.sum(weight * (real_part * real_part + imag_part * imag_part))
    summed = lax.psum(partial_term, ("pairs", "cols"))
    moment = summed / float(levels * levels * col_count * lax.axis_size("cols") * levels * THIRD)
    return (evolved, moment.reshape(1))


def solution(mesh):
    placed = (P(None, "pairs", None, "cols"), P(None, None, "cols"), P(), P("cols"))
    return jax.shard_map(
        local,
        mesh=mesh,
        in_specs=placed,
        out_specs=(P(None, "pairs", None, "cols"), P()),
        check_vma=False,
    )
```

profile of v0, /device:TPU:1, one launch (start us, length us, event | category | flops | bytes accessed | tf_op | source)
XLA Modules:
  0.0 395.6 jit_solution(17575144907077907084)
XLA Ops:
  7.2 0.8 constant_dynamic-slice_fusion
  8.0 0.1 reshape_squeeze.9
  8.1 0.1 copy.22
  8.2 0.1 copy.23
  8.3 3.2 copy.41
  11.5 8.5 %gather_fusion = f32[128,2,4096]{2,1,0:T(2,128)} fusion(f32[2,64,4096]{2,0,1:T(2,128)S(1)} %bitcast.62, s32[1024]{0:T(1024)S(1)} %pad_clamp_fusion.3), kind=kCustom, calls=%fused_computation.2 | custom fusion | bytes 8389120 | tf_op jit(solution)/shard_map/jit(_take)/gather | solution.py:71
  20.0 8.1 %broadcast_select_fusion.2 = f32[2,64,2,4096]{3,0,2,1:T(2,128)} fusion(f32[2,64,2,4096]{3,0,2,1:T(2,128)} %bitcast.63, pred[64,2]{1,0:T(8,128)(4,1)S(1)} %copy.23), kind=kLoop, calls=%fused_computation.9 | loop fusion | flops 1048576 | bytes 8388736 | tf_op jit(solution)/shard_map/jit(_take)/select_n | solution.py:71
  28.1 13.3 %all-to-all-start = ((f32[2,64,2,4096]{3,0,2,1:T(2,128)}), f32[2,64,2,4096]{3,0,2,1:T(2,128)}, u32[]{:S(2)}, u32[]{:S(2)}) async-start(f32[2,64,2,4096]{3,0,2,1:T(2,128)} %broadcast_select_fusion.2), calls=%async_computation | async-start | bytes 8388608 | tf_op jit(solution)/shard_map/all_to_all | solution.py:80
  41.5 12.2 %all-gather.2.cloned.1.call-start = ((), (), s32[]{:S(2)}) async-start(), calls=%async_computation.2 | async-start | bytes 2621440 | tf_op jit(solution)/shard_map/all_gather | solution.py:59
  53.7 0.0 all-gather.2.cloned.1.call-update
  53.7 0.9 dynamic-slice_maximum_fusion
  54.6 0.1 reshape.309
  54.6 0.1 reshape_squeeze.10
  54.8 0.7 compare_and_fusion.1
  55.5 32.4 %all-gather.2.cloned.1.call-done = f32[127,64,64]{0,2,1:T(8,128)} async-done(((f32[127,64,16]{0,2,1:T(8,128)}), f32[127,64,64]{0,2,1:T(8,128)}) %all-gather.2.cloned.1.call-update) | async-done | bytes 2080784 | tf_op jit(solution)/shard_map/all_gather | solution.py:59
  87.9 5.6 %copy.26 = f32[127,64,64]{2,1,0:T(8,128)} copy(f32[127,64,64]{0,2,1:T(8,128)} %all-gather.2.cloned.1.call-done) | data formatting | bytes 4161536 | tf_op jit(solution)/shard_map/all_gather | solution.py:59
  93.5 3.2 reshape.277
  96.8 45.5 %gather_fusion.1 = f32[8192]{0:T(1024)S(1)} fusion(f32[520192]{0:T(1024)S(1)} %reshape.277, s32[8192]{0:T(1024)S(1)} %broadcast_clamp_fusion), kind=kCustom, calls=%fused_computation.3 | custom fusion | bytes 98304 | tf_op jit(solution)/shard_map/jit(_take)/gather | solution.py:77
  142.3 0.1 reshape.308
  142.4 0.0 all-to-all-done
  142.4 10.5 %gather_fusion.3 = f32[128,2,4096]{2,1,0:T(2,128)} fusion(f32[2,128,4096]{2,0,1:T(2,128)} %bitcast.9, s32[1024]{0:T(1024)S(1)} %pad_clamp_fusion.2), kind=kCustom, calls=%fused_computation.clone | custom fusion | bytes 8389120 | tf_op jit(solution)/shard_map/jit(_take)/gather | solution.py:82
  152.9 4.9 %broadcast_select_fusion.1 = f32[128,2,4096]{2,1,0:T(2,128)S(1)} fusion(f32[128,2,4096]{2,1,0:T(2,128)} %gather_fusion.3, pred[128]{0:T(512)(128)(4,1)S(1)} %get-tuple-element.7), kind=kLoop, calls=%fused_computation.8 | loop fusion | flops 1048576 | bytes 8388736 | tf_op jit(solution)/shard_map/jit(_take)/select_n | solution.py:82
  157.8 7.3 %convolution_bitcast_fusion = f32[2,2,64,4096]{3,2,0,1:T(8,128)S(1)} fusion(f32[2,2,64,4096]{3,0,2,1:T(2,128)S(1)} %bitcast.65, f32[2,64,64]{2,1,0:T(8,128)S(1)} %reshape.308, s32[64,2,64,64]{3,2,1,0:T(8,128)} %constant.132.clone, s32[]{:T(128)S(6)} %select_n.99), kind=kOutput, calls=%fused_computation.5 | convolution fusion | flops 805347328 | bytes 8486916 | tf_op jit(solution)/shard_map/gij,pgjc->pgic/dot_general | solution.py:84
  165.1 0.4 copy.28
  165.5 5.4 %copy.29 = f32[2,128,4096]{2,0,1:T(2,128)} copy(f32[2,128,4096]{2,1,0:T(8,128)S(1)} %bitcast.66) | data formatting | bytes 8388608 | tf_op jit(solution)/shard_map/reshape | solution.py:85
  170.9 10.5 %gather_fusion.4 = f32[128,2,4096]{2,1,0:T(2,128)} fusion(f32[2,128,4096]{2,0,1:T(2,128)} %copy.29, s32[1024]{0:T(1024)S(1)} %pad_clamp_fusion.1), kind=kCustom, calls=%fused_computation.1.clone | custom fusion | bytes 8389120 | tf_op jit(solution)/shard_map/jit(_take)/gather | solution.py:85
  181.4 8.2 %broadcast_select_fusion = f32[128,2,4096]{2,1,0:T(2,128)} fusion(f32[128,2,4096]{2,1,0:T(2,128)} %gather_fusion.4, pred[128]{0:T(512)(128)(4,1)S(1)} %compare_and_fusion), kind=kLoop, calls=%fused_computation.7 | loop fusion | flops 1048576 | bytes 8388736 | tf_op jit(solution)/shard_map/jit(_take)/select_n | solution.py:85
  189.5 0.0 copy-start.1
  189.5 11.5 %all-to-all-start.1 = ((f32[2,64,2,4096]{3,0,2,1:T(2,128)}), f32[2,64,2,4096]{3,0,2,1:T(2,128)}, u32[]{:S(2)}, u32[]{:S(2)}) async-start(f32[2,64,2,4096]{3,0,2,1:T(2,128)} %bitcast.64), calls=%async_computation.1 | async-start | bytes 8388608 | tf_op jit(solution)/shard_map/all_to_all | solution.py:87
  201.1 0.7 fusion.33
  201.8 0.7 compare_and_fusion.3
  202.5 0.0 copy-done.1
  202.5 0.6 fusion.37
  203.1 1.3 fusion.28
  204.4 91.4 %all-to-all-done.1 = f32[2,64,2,4096]{3,0,2,1:T(2,128)} async-done(((f32[2,64,2,4096]{3,0,2,1:T(2,128)}), f32[2,64,2,4096]{3,0,2,1:T(2,128)}, u32[]{:S(2)}, u32[]{:S(2)}) %all-to-all-start.1) | async-done | bytes 4194336 | tf_op jit(solution)/shard_map/all_to_all | solution.py:87
  295.8 6.2 %gather_fusion.2 = f32[64,2,4096]{2,1,0:T(2,128)} fusion(f32[2,128,4096]{2,0,1:T(2,128)} %bitcast.20, s32[1024]{0:T(1024)S(1)} %pad_clamp_fusion), kind=kCustom, calls=%fused_computation.4 | custom fusion | bytes 4194560 | tf_op jit(solution)/shard_map/jit(_take)/gather | solution.py:88
  302.0 0.0 copy-start
  302.0 2.9 fusion.1
  304.9 1.0 fusion.8
  305.9 0.0 copy-done
  305.9 75.2 %psum.7 = f32[]{:T(128)} all-reduce(f32[]{:T(128)} %fusion.8), channel_id=1, replica_groups=mesh['pairs'=64,'cols'=4] {'pairs','cols'}, use_global_device_ids=true, to_apply=%region_1.3 | all-reduce | flops 1 | bytes 8 | tf_op jit(solution)/shard_map/psum | solution.py:110
  381.7 4.0 %fusion.6 = (f32[1,64,4096]{2,1,0:T(8,128)S(1)}, f32[1,64,4096]{2,1,0:T(8,128)S(1)}) fusion(f32[2,64,4096]{2,1,0:T(8,128)S(1)} %fusion.1, f32[4096]{0:T(1024)S(1)} %convert_element_type.29, f32[64]{0:T(128)S(1)} %fusion.28), kind=kLoop, calls=%fused_computation.20 | loop fusion | flops 1835008 | bytes 4210944 | tf_op jit(solution)/shard_map/sub | solution.py:103
  385.8 1.5 maximum_bitcast_fusion
  (12 shorter events, 0.1 us)
Async XLA Ops:
  28.1 114.3 %all-to-all-start = ((f32[2,64,2,4096]{3,0,2,1:T(2,128)}), f32[2,64,2,4096]{3,0,2,1:T(2,128)}, u32[]{:S(2)}, u32[]{:S(2)}) async-start(f32[2,64,2,4096]{3,0,2,1:T(2,128)} %broadcast_select_fusion.2), calls=%async_computation | async-start | bytes 8388608 | tf_op jit(solution)/shard_map/all_to_all | solution.py:80
  41.5 46.5 %all-gather.2.cloned.1.call-start = ((), (), s32[]{:S(2)}) async-start(), calls=%async_computation.2 | async-start | bytes 2621440 | tf_op jit(solution)/shard_map/all_gather | solution.py:59
  189.5 13.0 %copy-start.1 = (f32[2]{0:T(128)S(1)}, f32[2]{0:T(128)}, u32[]{:S(2)}) copy-start(f32[2]{0:T(128)} %param.13) | copy-start | bytes 28
  189.5 106.2 %all-to-all-start.1 = ((f32[2,64,2,4096]{3,0,2,1:T(2,128)}), f32[2,64,2,4096]{3,0,2,1:T(2,128)}, u32[]{:S(2)}, u32[]{:S(2)}) async-start(f32[2,64,2,4096]{3,0,2,1:T(2,128)} %bitcast.64), calls=%async_computation.1 | async-start | bytes 8388608 | tf_op jit(solution)/shard_map/all_to_all | solution.py:87
  302.0 4.0 %copy-start = (s32[4096]{0:T(1024)S(1)}, s32[4096]{0:T(1024)}, u32[]{:S(2)}) copy-start(s32[4096]{0:T(1024)} %param.14) | copy-start | bytes 49156
Sparse Core Ops, SparseCore 0:
  53.8 34.0 all-gather.1
where the time goes:
time: 403 us; the launch traced here: 396 us
  waiting for transfers between devices  124 us (31%)
  local copies, waits for them, and re-layouts  101 us (25%)
  blocking collectives  75.2 us (19%)
  starting transfers between devices  37.1 us (9%)
  other arithmetic  35 us (9%)
  between operations  16.4 us (4%)
  matrix products  7.27 us (2%)
    all_to_all x1, waiting for transfers between devices, local(): lax.all_to_all(leaving, 'pairs', split_axis=1, concat_axis=1, tiled=True)  91.4 us
    psum x1, blocking collectives, local(): summed = lax.psum(partial_term, ('pairs', 'cols'))  75.2 us
    gather x2, local copies, waits for them, and re-layouts, local(): jnp.take(flat_mix, jnp.maximum(my_mat, 0))  45.6 us
    all_gather x1, waiting for transfers between devices, local(): full_mix = lax.all_gather(sector_mix, 'cols', axis=2, tiled=True)  32.4 us
    all_to_all x1, starting transfers between devices, local(): lax.all_to_all(outgoing, 'pairs', split_axis=1, concat_axis=1, tiled=True)  13.3 us
    all_gather x1, starting transfers between devices, local(): full_mix = lax.all_gather(sector_mix, 'cols', axis=2, tiled=True)  12.2 us
    all_to_all x1, starting transfers between devices, local(): lax.all_to_all(leaving, 'pairs', split_axis=1, concat_axis=1, tiled=True)  11.5 us
    gather x1, local copies, waits for them, and re-layouts, local(): jnp.take(combined.reshape(2, groups * levels, item_count), my_back, axis=1)  10.5 us
  transfers between devices with their start and end apart: 3, of which 2 were waited for; matrix products, arithmetic and copies ran while one was open for 15% of the time, Pallas kernels for 0%

commit v1 on v0

v1 whole, which is shorter than its diff:
```python
import functools

import jax
import jax.numpy as jnp
from jax import lax
from jax.experimental import pallas as pl
from jax.experimental.pallas import tpu as pltpu
from jax.sharding import PartitionSpec as P

THIRD = 64
MEMB = 128
WINDOW = 2
LEVELS = 64
LANES = 128
CHUNKS = 2


def blend(low, high, shift):
    sub = lax.broadcasted_iota(jnp.int32, low.shape, 0)
    return jnp.where(sub < shift, low, high)


def pack_kernel(x_ref, out_ref):
    blocks = x_ref.shape[2] // LANES
    lines = 2 * blocks
    n1 = lax.axis_index("pairs")
    tile, shift = n1 // 8, n1 % 8
    for part in range(2):
        for j in range(blocks):
            lanes = slice(j * LANES, (j + 1) * LANES)
            turned = [
                pltpu.roll(x_ref[part, 8 * a : 8 * a + 8, lanes], shift, 0) for a in range(LEVELS // 8)
            ]
            for a in range(LEVELS // 8):
                slot = 8 * ((a + tile) % 8)
                out_ref[pl.ds(slot * lines + part * blocks + j, 8, stride=lines), :] = blend(
                    turned[a - 1], turned[a], shift
                )


def mix_kernel(first_col, x_ref, pieces_ref, out_ref, moment_ref):
    lines = out_ref.shape[0] // LEVELS
    blocks = lines // 2
    owner = lax.axis_index("pairs")
    base = lax.axis_index("cols") * (4096 // 256)
    row = lax.broadcasted_iota(jnp.int32, (LEVELS, LANES), 0)
    col = lax.broadcasted_iota(jnp.int32, (LEVELS, LANES), 1)
    low = pieces_ref[0]
    high = pltpu.roll(pltpu.roll(pieces_ref[1], owner + 1, 0), owner + 1, 1)
    zero = jnp.zeros_like(low)
    low = jnp.where((row <= owner) & (col <= owner), low, zero)
    high = jnp.where((row > owner) & (col > owner) & (col < LEVELS), high, zero)
    matrix = (low + high)[:, :LEVELS]
    total = jnp.zeros((LEVELS, LANES), jnp.float32)
    for line in range(lines):
        mixed = jnp.dot(
            matrix,
            x_ref[pl.ds(line, LEVELS, stride=lines), :],
            precision=lax.Precision.HIGHEST,
            preferred_element_type=jnp.float32,
        )
        out_ref[pl.ds(line, LEVELS, stride=lines), :] = mixed
        third = base + (first_col + (line % blocks) * LANES) // (MEMB * WINDOW)
        total += (third + 1).astype(jnp.float32) * (mixed * mixed)
    moment_ref[...] = jnp.sum(total * (row + 1).astype(jnp.float32), axis=0, keepdims=True)


def turn_kernel(first, x_ref, cos_ref, sin_ref, *refs):
    out_ref = refs[-1]
    blocks = out_ref.shape[2] // LANES
    lines = 2 * blocks
    n1 = lax.axis_index("pairs")
    tile, shift = n1 // 8, n1 % 8
    back = (8 - shift) % 8

    def rows(part, j):
        turned = []
        for a in range(LEVELS // 8 + 1):
            slot = 8 * ((a + tile) % 8)
            turned.append(
                pltpu.roll(x_ref[pl.ds(slot * lines + part * blocks + j, 8, stride=lines), :], back, 0)
            )
        return [blend(turned[a], turned[a + 1], 8 - shift) for a in range(LEVELS // 8)]

    for j in range(blocks):
        lanes = slice(j * LANES, (j + 1) * LANES)
        real, imag = rows(0, j), rows(1, j)
        for a in range(LEVELS // 8):
            span = slice(8 * a, 8 * a + 8)
            cosine, sine = cos_ref[span, lanes], sin_ref[span, lanes]
            out_ref[0, span, lanes] = cosine * real[a] - sine * imag[a]
            out_ref[1, span, lanes] = sine * real[a] + cosine * imag[a]


def local(state, sector_mix, kerr_rates, column_load):
    pair_count = lax.axis_size("pairs")
    col_devices = lax.axis_size("cols")
    device = lax.axis_index("pairs")
    col_device = lax.axis_index("cols")
    levels, col_count = state.shape[2], state.shape[3]
    assert pair_count == levels == LEVELS and state.shape[1] == 1
    state = state.reshape(2, levels, col_count)
    width = col_count // CHUNKS
    blocks = width // LANES
    lines = 2 * blocks
    size = levels * lines
    vmem = pl.BlockSpec(memory_space=pltpu.VMEM)

    def exchange(rows):
        rows = rows.reshape(levels, lines, LANES)
        return lax.all_to_all(rows, "pairs", 0, 0, tiled=True).reshape(size, LANES)

    low = lax.dynamic_slice_in_dim(sector_mix, device, 1, 0)
    high = lax.dynamic_slice_in_dim(sector_mix, jnp.minimum(device + levels, 2 * levels - 2), 1, 0)
    mine = jnp.concatenate([low, high], 0)
    share = mine.shape[2]
    pieces = jnp.zeros((2, levels, LANES), jnp.float32)
    for step in range(col_devices):
        ring = [(i, (i + step) % col_devices) for i in range(col_devices)]
        part = lax.ppermute(mine, "cols", ring) if step else mine
        owner = (col_device - step) % col_devices
        pieces = lax.dynamic_update_slice(pieces, part, (0, 0, owner * share))

    packed = []
    for chunk in range(CHUNKS):
        packed.append(
            pl.pallas_call(
                pack_kernel,
                grid=(1,),
                in_specs=[pl.BlockSpec((2, levels, width), functools.partial(lambda c, i: (0, 0, c), chunk))],
                out_specs=pl.BlockSpec((size, LANES), lambda i: (0, 0)),
                out_shape=jax.ShapeDtypeStruct((size, LANES), jnp.float32),
                cost_estimate=pl.CostEstimate(flops=0, bytes_accessed=16 * levels * width, transcendentals=0),
                name="pack",
            )(state)
        )
    arrived = [exchange(p) for p in packed]

    n1 = device.astype(jnp.float32)
    n2 = jnp.arange(levels).astype(jnp.float32)
    phases = (kerr_rates[0] * n1 + kerr_rates[1] * n2)[:, None] * column_load.astype(jnp.float32)[None, :]
    cosine, sine = jnp.cos(phases), jnp.sin(phases)

    returned = []
    moments = []
    for chunk in range(CHUNKS):
        mixed, moment = pl.pallas_call(
            functools.partial(mix_kernel, chunk * width),
            in_specs=[vmem, vmem],
            out_specs=[vmem, vmem],
            out_shape=[
                jax.ShapeDtypeStruct((size, LANES), jnp.float32),
                jax.ShapeDtypeStruct((1, LANES), jnp.float32),
            ],
            cost_estimate=pl.CostEstimate(
                flops=12 * levels * size * LANES, bytes_accessed=16 * levels * width, transcendentals=0
            ),
            name="mix",
        )(arrived[chunk], pieces)
        moments.append(moment)
        returned.append(exchange(mixed))

    summed = lax.psum(jnp.sum(sum(moments)), ("pairs", "cols"))
    moment = summed / float(levels * levels * col_count * col_devices * levels * THIRD)

    evolved = None
    for chunk in range(CHUNKS):
        table = pl.BlockSpec((levels, width), functools.partial(lambda c, i: (0, c), chunk))
        inputs = [returned[chunk], cosine, sine]
        specs = [pl.BlockSpec((size, LANES), lambda i: (0, 0)), table, table]
        if chunk:
            inputs.append(evolved)
            specs.append(pl.BlockSpec(memory_space=pl.ANY))
        evolved = pl.pallas_call(
            functools.partial(turn_kernel, not chunk),
            grid=(1,),
            in_specs=specs,
            out_specs=pl.BlockSpec((2, levels, width), functools.partial(lambda c, i: (0, 0, c), chunk)),
            out_shape=jax.ShapeDtypeStruct((2, levels, col_count), jnp.float32),
            input_output_aliases={3: 0} if chunk else {},
            cost_estimate=pl.CostEstimate(flops=0, bytes_accessed=24 * levels * width, transcendentals=0),
            name="turn",
        )(*inputs)
    return evolved.reshape(2, 1, levels, col_count), moment.reshape(1)


def solution(mesh):
    placed = (P(None, "pairs", None, "cols"), P(None, None, "cols"), P(), P("cols"))
    return jax.shard_map(
        local,
        mesh=mesh,
        in_specs=placed,
        out_specs=(P(None, "pairs", None, "cols"), P()),
        check_vma=False,
    )
```

time: 403 us -> 216 us (0.54); the launches traced: 396 us -> 215 us
  local copies, waits for them, and re-layouts: 101 us -> 7.12 us
  waiting for transfers between devices: 124 us -> 62.4 us
  other arithmetic: 35 us -> 5.97 us
  Pallas kernels: 0 us -> 21.2 us
  between operations: 16.4 us -> 3.27 us
  matrix products: 7.27 us -> 0 us
    gather x6 -> x0, local copies, waits for them, and re-layouts: 81.2 us -> none  [the longest x2 45.6 us: local(): jnp.take(flat_mix, jnp.maximum(my_mat, 0))]
    all_gather x1 -> x0, waiting for transfers between devices: 32.4 us -> none  [local(): full_mix = lax.all_gather(sector_mix, 'cols', axis=2, tiled=True)]
    all_to_all x2 -> x4, waiting for transfers between devices: 91.4 us -> 61.4 us  [exchange(): return lax.all_to_all(rows, 'pairs', 0, 0, tiled=True).reshape(size, LANES)]
    select_n x7 -> x0, other arithmetic: 24.8 us -> none  [the longest x2 8.16 us: local(): jnp.take(combined.reshape(2, groups * levels, item_count), my_back, axis=1)]
    pallas_call x0 -> x6, Pallas kernels: none -> 21.2 us  [the longest x2 8.27 us: local(): pl.pallas_call(functools.partial(mix_kernel, chunk * width), in_specs=[vm...]
    all_gather x1 -> x0, starting transfers between devices: 12.2 us -> none  [local(): full_mix = lax.all_gather(sector_mix, 'cols', axis=2, tiled=True)]
    reshape x2 -> x0, local copies, waits for them, and re-layouts: 8.61 us -> none  [the longest x1 5.36 us: local(): combined.reshape(2, groups * levels, item_count)]
    dot_general x1 -> x0, matrix products: 7.27 us -> none  [local(): jnp.einsum('gij,pgjc->pgic', blocks, gathered, precision=lax.Precision.HI...]
  transfers between devices with their start and end apart: 3 -> 7, of which waited for: 2 -> 4; matrix products, arithmetic and copies ran while one was open for 15% -> 5% of each run, Pallas kernels for 0% -> 7%
where the time goes in v1:
time: 216 us; the launch traced here: 215 us
  blocking collectives  78.3 us (36%)
  waiting for transfers between devices  62.4 us (29%)
  starting transfers between devices  36.8 us (17%)
  Pallas kernels  21.2 us (10%)
  local copies, waits for them, and re-layouts  7.12 us (3%)
  other arithmetic  5.97 us (3%)
  between operations  3.27 us (2%)
    psum x1, blocking collectives, local(): summed = lax.psum(jnp.sum(sum(moments)), ('pairs', 'cols'))  78.3 us
    all_to_all x4, waiting for transfers between devices, exchange(): return lax.all_to_all(rows, 'pairs', 0, 0, tiled=True).reshape(size, LANES)  61.4 us
    all_to_all x4, starting transfers between devices, exchange(): return lax.all_to_all(rows, 'pairs', 0, 0, tiled=True).reshape(size, LANES)  32 us
    pallas_call x2, Pallas kernels, local(): pl.pallas_call(functools.partial(mix_kernel, chunk * width), in_specs=[vm...  8.27 us
    pallas_call x2, Pallas kernels, local(): pl.pallas_call(pack_kernel, grid=(1,), in_specs=[pl.BlockSpec((2, levels,...  6.6 us
    pallas_call x2, Pallas kernels, local(): pl.pallas_call(functools.partial(turn_kernel, not chunk), grid=(1,), in_s...  6.38 us
    ppermute x3, starting transfers between devices, local(): part = lax.ppermute(mine, 'cols', ring) if step else mine  4.85 us
    sin x1, other arithmetic, local(): cosine, sine = (jnp.cos(phases), jnp.sin(phases))  4.79 us
  transfers between devices with their start and end apart: 7, of which 4 were waited for; matrix products, arithmetic and copies ran while one was open for 5% of the time, Pallas kernels for 7%

profile of v1, /device:TPU:1, one launch (start us, length us, event | category | flops | bytes accessed | tf_op | source)
XLA Modules:
  0.0 215.1 jit_solution(17419465397803489492)
XLA Ops:
  0.6 3.3 %pack.3 = f32[2048,128]{1,0:T(8,128)} custom-call(f32[2,64,4096]{2,1,0:T(8,128)} %bitcast.16), custom_call_target="tpu_custom_call" | custom-call | bytes 2097152 | tf_op jit(solution)/shard_map/pack/pallas_call | solution.py:127
  3.9 13.1 %all-to-all-start.2 = ((f32[64,32,128]{2,1,0:T(8,128)}), f32[64,32,128]{2,1,0:T(8,128)S(1)}, u32[]{:S(2)}, u32[]{:S(2)}) async-start(f32[64,32,128]{2,1,0:T(8,128)} %bitcast.21), calls=%async_computation.2 | async-start | bytes 2097152 | tf_op jit(solution)/shard_map/all_to_all | solution.py:111
  17.1 0.0 copy-start.4
  17.1 3.3 %pack.2 = f32[2048,128]{1,0:T(8,128)} custom-call(f32[2,64,4096]{2,1,0:T(8,128)} %bitcast.17), custom_call_target="tpu_custom_call" | custom-call | bytes 2097152 | tf_op jit(solution)/shard_map/pack/pallas_call | solution.py:127
  20.4 24.8 %all-to-all-done.2 = f32[64,32,128]{2,1,0:T(8,128)S(1)} async-done(((f32[64,32,128]{2,1,0:T(8,128)}), f32[64,32,128]{2,1,0:T(8,128)S(1)}, u32[]{:S(2)}, u32[]{:S(2)}) %all-to-all-start.2) | async-done | bytes 1048608 | tf_op jit(solution)/shard_map/all_to_all | solution.py:111
  45.2 6.3 %all-to-all-start = ((f32[64,32,128]{2,1,0:T(8,128)}), f32[64,32,128]{2,1,0:T(8,128)S(1)}, u32[]{:S(2)}, u32[]{:S(2)}) async-start(f32[64,32,128]{2,1,0:T(8,128)} %bitcast.18), calls=%async_computation | async-start | bytes 2097152 | tf_op jit(solution)/shard_map/all_to_all | solution.py:111
  51.5 0.0 copy-done.4
  51.5 1.1 constant_dynamic-slice_fusion.1
  52.7 0.0 copy-done.3
  52.7 1.3 copy.17
  54.0 0.3 copy.18
  54.2 0.1 copy.12
  54.3 1.2 collective-permute-start
  55.6 2.5 %collective-permute-start.1 = (f32[2,64,16]{2,1,0:T(8,128)S(1)}, f32[2,64,16]{2,1,0:T(8,128)S(1)}, u32[]{:S(2)}, u32[]{:S(2)}) collective-permute-start(f32[2,64,16]{2,1,0:T(8,128)S(1)} %copy.12), channel_id=1, source_target_pairs={{0,2},{1,3},{2,0},{3,1},{4,6},{5,7},{6,4},{7,5},{8,10},{9,11},{10,... | collective-permute-start | bytes 24584 | tf_op jit(solution)/shard_map/ppermute | solution.py:120
  58.0 1.2 collective-permute-start.2
  59.2 0.3 dynamic_update_slice.12
  59.5 0.0 collective-permute-done
  59.5 0.6 dynamic_update_slice.13
  60.1 1.0 collective-permute-done.1
  61.2 0.6 dynamic_update_slice.14
  61.7 0.0 collective-permute-done.2
  61.7 0.6 dynamic_update_slice.15.pieces_ref
  62.4 0.0 copy-start.5
  62.4 0.6 copy-done.5
  63.0 4.1 %mix.3 = (f32[2048,128]{1,0:T(8,128)}, f32[1,128]{1,0:T(1,128)}) custom-call(f32[2048,128]{1,0:T(8,128)} %bitcast.23, f32[2,64,128]{2,1,0:T(8,128)} %copy-done.5), custom_call_target="tpu_custom_call" | custom-call | flops 201326592 | bytes 2097152 | tf_op jit(solution)/shard_map/mix/pallas_call | solution.py:147
  67.1 12.5 %all-to-all-done = f32[64,32,128]{2,1,0:T(8,128)S(1)} async-done(((f32[64,32,128]{2,1,0:T(8,128)}), f32[64,32,128]{2,1,0:T(8,128)S(1)}, u32[]{:S(2)}, u32[]{:S(2)}) %all-to-all-start) | async-done | bytes 1048608 | tf_op jit(solution)/shard_map/all_to_all | solution.py:111
  79.7 6.3 %all-to-all-start.3 = ((f32[64,32,128]{2,1,0:T(8,128)}), f32[64,32,128]{2,1,0:T(8,128)S(1)}, u32[]{:S(2)}, u32[]{:S(2)}) async-start(f32[64,32,128]{2,1,0:T(8,128)} %bitcast.25), calls=%async_computation.3 | async-start | bytes 2097152 | tf_op jit(solution)/shard_map/all_to_all | solution.py:111
  86.0 0.0 copy-start.6
  86.0 0.0 copy-start.7
  86.0 0.0 copy-start.8
  86.0 0.0 copy-done.2
  86.0 4.1 %mix.2 = (f32[2048,128]{1,0:T(8,128)}, f32[1,128]{1,0:T(1,128)}) custom-call(f32[2048,128]{1,0:T(8,128)} %bitcast.22, f32[2,64,128]{2,1,0:T(8,128)} %copy-done.5), custom_call_target="tpu_custom_call" | custom-call | flops 201326592 | bytes 2097152 | tf_op jit(solution)/shard_map/mix/pallas_call | solution.py:147
  90.1 24.0 %all-to-all-done.3 = f32[64,32,128]{2,1,0:T(8,128)S(1)} async-done(((f32[64,32,128]{2,1,0:T(8,128)}), f32[64,32,128]{2,1,0:T(8,128)S(1)}, u32[]{:S(2)}, u32[]{:S(2)}) %all-to-all-start.3) | async-done | bytes 1048608 | tf_op jit(solution)/shard_map/all_to_all | solution.py:111
  114.1 6.3 %all-to-all-start.1 = ((f32[64,32,128]{2,1,0:T(8,128)}), f32[64,32,128]{2,1,0:T(8,128)S(1)}, u32[]{:S(2)}, u32[]{:S(2)}) async-start(f32[64,32,128]{2,1,0:T(8,128)} %bitcast.24), calls=%async_computation.1 | async-start | bytes 2097152 | tf_op jit(solution)/shard_map/all_to_all | solution.py:111
  120.4 0.0 copy-done.6
  120.4 0.0 copy-done.7
  120.4 0.6 fusion
  121.7 0.6 multiply_add_fusion
  122.2 0.0 copy-done.8
  122.2 0.0 copy-done.9
  122.3 0.6 add_reduce_fusion
  122.9 4.8 %multiply_sine_fusion = (f32[64,4096]{1,0:T(8,128)}, f32[64,4096]{1,0:T(8,128)}) fusion(f32[4096]{0:T(1024)S(1)} %convert_element_type.15, f32[64]{0:T(128)S(1)} %multiply_add_fusion), kind=kLoop, calls=%fused_computation | loop fusion | flops 262144 | bytes 2113792 | tf_op jit(solution)/shard_map/sin | solution.py:142
  127.6 0.0 copy-done
  127.7 78.3 %psum.7 = f32[]{:T(128)} all-reduce(f32[]{:T(128)} %add_reduce_fusion), channel_id=1, replica_groups=mesh['pairs'=64,'cols'=4] {'pairs','cols'}, use_global_device_ids=true, to_apply=%region_1.2 | all-reduce | flops 1 | bytes 8 | tf_op jit(solution)/shard_map/psum | solution.py:163
  206.6 3.2 %turn.2.refs_0_ = f32[2,64,4096]{2,1,0:T(8,128)} custom-call(f32[2048,128]{1,0:T(8,128)} %bitcast.19, f32[64,4096]{1,0:T(8,128)} %get-tuple-element.17.cos_ref, f32[64,4096]{1,0:T(8,128)} %get-tuple-element.16.sin_ref), custom_call_target="tpu_custom_call" | custom-call | bytes 3145728 | tf_op jit(solution)/shard_map/turn/pallas_call | solution.py:174
  209.8 0.0 all-to-all-done.1
  209.8 1.0 copy-done.1
  210.8 3.2 %turn.3 = f32[2,64,4096]{2,1,0:T(8,128)} custom-call(f32[2048,128]{1,0:T(8,128)} %bitcast.20, f32[64,4096]{1,0:T(8,128)} %get-tuple-element.17.cos_ref, f32[64,4096]{1,0:T(8,128)} %get-tuple-element.16.sin_ref, f32[2,64,4096]{2,1,0:T(8,128)} %turn.2.refs_0_), custom_call_target="tpu_custom_call", output_to_operand_aliasing={{}: (3, {})} | custom-call | bytes 3145728 | tf_op jit(solution)/shard_map/turn/pallas_call | solution.py:174
  (8 shorter events, 0.0 us)
Async XLA Ops:
  3.9 41.3 %all-to-all-start.2 = ((f32[64,32,128]{2,1,0:T(8,128)}), f32[64,32,128]{2,1,0:T(8,128)S(1)}, u32[]{:S(2)}, u32[]{:S(2)}) async-start(f32[64,32,128]{2,1,0:T(8,128)} %bitcast.21), calls=%async_computation.2 | async-start | bytes 2097152 | tf_op jit(solution)/shard_map/all_to_all | solution.py:111
  17.1 34.5 %copy-start.4 = (f32[127,64,16]{0,2,1:T(8,128)S(1)}, f32[127,64,16]{0,2,1:T(8,128)}, u32[]{:S(2)}) copy-start(f32[127,64,16]{0,2,1:T(8,128)} %param.5) | copy-start | bytes 1560580
  45.2 7.4 %copy-start.3 = (f32[64,32,128]{2,1,0:T(8,128)}, f32[64,32,128]{2,1,0:T(8,128)S(1)}, u32[]{:S(2)}) copy-start(f32[64,32,128]{2,1,0:T(8,128)S(1)} %all-to-all-done.2) | copy-start | bytes 3145732
  45.2 34.4 %all-to-all-start = ((f32[64,32,128]{2,1,0:T(8,128)}), f32[64,32,128]{2,1,0:T(8,128)S(1)}, u32[]{:S(2)}, u32[]{:S(2)}) async-start(f32[64,32,128]{2,1,0:T(8,128)} %bitcast.18), calls=%async_computation | async-start | bytes 2097152 | tf_op jit(solution)/shard_map/all_to_all | solution.py:111
  54.3 5.1 %collective-permute-start = (f32[2,64,16]{2,1,0:T(8,128)S(1)}, f32[2,64,16]{2,1,0:T(8,128)S(1)}, u32[]{:S(2)}, u32[]{:S(2)}) collective-permute-start(f32[2,64,16]{2,1,0:T(8,128)S(1)} %copy.12), channel_id=1, source_target_pairs={{0,1},{1,2},{2,3},{3,0},{4,5},{5,6},{6,7},{7,4},{8,9},{9,10},{10,1... | collective-permute-start | bytes 24584 | tf_op jit(solution)/shard_map/ppermute | solution.py:120
  55.6 5.6 %collective-permute-start.1 = (f32[2,64,16]{2,1,0:T(8,128)S(1)}, f32[2,64,16]{2,1,0:T(8,128)S(1)}, u32[]{:S(2)}, u32[]{:S(2)}) collective-permute-start(f32[2,64,16]{2,1,0:T(8,128)S(1)} %copy.12), channel_id=1, source_target_pairs={{0,2},{1,3},{2,0},{3,1},{4,6},{5,7},{6,4},{7,5},{8,10},{9,11},{10,... | collective-permute-start | bytes 24584 | tf_op jit(solution)/shard_map/ppermute | solution.py:120
  58.0 3.7 %collective-permute-start.2 = (f32[2,64,16]{2,1,0:T(8,128)S(1)}, f32[2,64,16]{2,1,0:T(8,128)S(1)}, u32[]{:S(2)}, u32[]{:S(2)}) collective-permute-start(f32[2,64,16]{2,1,0:T(8,128)S(1)} %copy.12), channel_id=1, source_target_pairs={{0,3},{1,0},{2,1},{3,2},{4,7},{5,4},{6,5},{7,6},{8,11},{9,8},{10,9... | collective-permute-start | bytes 24584 | tf_op jit(solution)/shard_map/ppermute | solution.py:120
  62.4 0.6 copy-start.5
  79.7 6.3 %copy-start.2 = (f32[64,32,128]{2,1,0:T(8,128)}, f32[64,32,128]{2,1,0:T(8,128)S(1)}, u32[]{:S(2)}) copy-start(f32[64,32,128]{2,1,0:T(8,128)S(1)} %all-to-all-done) | copy-start | bytes 3145732
  79.7 34.4 %all-to-all-start.3 = ((f32[64,32,128]{2,1,0:T(8,128)}), f32[64,32,128]{2,1,0:T(8,128)S(1)}, u32[]{:S(2)}, u32[]{:S(2)}) async-start(f32[64,32,128]{2,1,0:T(8,128)} %bitcast.25), calls=%async_computation.3 | async-start | bytes 2097152 | tf_op jit(solution)/shard_map/all_to_all | solution.py:111
  86.0 34.5 %copy-start.6 = (s32[4096]{0:T(1024)S(1)}, s32[4096]{0:T(1024)}, u32[]{:S(2)}) copy-start(s32[4096]{0:T(1024)} %param.7) | copy-start | bytes 49156
  86.0 34.5 %copy-start.7 = (f32[2]{0:T(128)S(1)}, f32[2]{0:T(128)}, u32[]{:S(2)}) copy-start(f32[2]{0:T(128)} %param.6) | copy-start | bytes 28
  86.0 36.3 %copy-start.8 = (f32[1,128]{1,0:T(1,128)S(1)}, f32[1,128]{1,0:T(1,128)}, u32[]{:S(2)}) copy-start(f32[1,128]{1,0:T(1,128)} %get-tuple-element.8) | copy-start | bytes 1540
  90.1 32.1 %copy-start.9 = (f32[1,128]{1,0:T(1,128)S(1)}, f32[1,128]{1,0:T(1,128)}, u32[]{:S(2)}) copy-start(f32[1,128]{1,0:T(1,128)} %get-tuple-element.9) | copy-start | bytes 1540
  114.1 13.5 %copy-start = (f32[64,32,128]{2,1,0:T(8,128)}, f32[64,32,128]{2,1,0:T(8,128)S(1)}, u32[]{:S(2)}) copy-start(f32[64,32,128]{2,1,0:T(8,128)S(1)} %all-to-all-done.3) | copy-start | bytes 3145732
  114.1 95.7 %all-to-all-start.1 = ((f32[64,32,128]{2,1,0:T(8,128)}), f32[64,32,128]{2,1,0:T(8,128)S(1)}, u32[]{:S(2)}, u32[]{:S(2)}) async-start(f32[64,32,128]{2,1,0:T(8,128)} %bitcast.24), calls=%async_computation.1 | async-start | bytes 2097152 | tf_op jit(solution)/shard_map/all_to_all | solution.py:111
  209.8 1.0 copy-start.1

commit v2 on v1

v2 whole, which is shorter than its diff:
```python
import functools

import jax
import jax.numpy as jnp
from jax import lax
from jax.experimental import pallas as pl
from jax.experimental.pallas import tpu as pltpu
from jax.sharding import PartitionSpec as P

THIRD = 64
MEMB = 128
WINDOW = 2
LEVELS = 64
LANES = 128
STEPS = 4
VMEM_LIMIT = 24 * 1024 * 1024


def blend(low, high, shift):
    sub = lax.broadcasted_iota(jnp.int32, low.shape, 0)
    return jnp.where(sub < shift, low, high)


def pack_kernel(x_ref, out_ref):
    blocks = x_ref.shape[2] // LANES
    lines = 2 * blocks
    flat = out_ref.reshape(LEVELS * lines, LANES)
    n1 = lax.axis_index("pairs")
    tile, shift = n1 // 8, n1 % 8
    for part in range(2):
        for j in range(blocks):
            lanes = slice(j * LANES, (j + 1) * LANES)
            turned = [
                pltpu.roll(x_ref[part, 8 * a : 8 * a + 8, lanes], shift, 0) for a in range(LEVELS // 8)
            ]
            for a in range(LEVELS // 8):
                slot = 8 * ((a + tile) % 8)
                flat[pl.ds(slot * lines + part * blocks + j, 8, stride=lines), :] = blend(
                    turned[a - 1], turned[a], shift
                )


def split(values):
    high = values.astype(jnp.bfloat16)
    return high, (values - high.astype(jnp.float32)).astype(jnp.bfloat16)


def mix_kernel(col_count, x_ref, pieces_ref, out_ref, moment_ref, matrix_ref):
    lines = x_ref.shape[1]
    source = x_ref.reshape(LEVELS * lines, LANES)
    target = out_ref.reshape(LEVELS * lines, LANES)
    step = pl.program_id(0)
    row = lax.broadcasted_iota(jnp.int32, (LEVELS, LANES), 0)

    @pl.when(step == 0)
    def _():
        owner = lax.axis_index("pairs")
        col = lax.broadcasted_iota(jnp.int32, (LEVELS, LANES), 1)
        low = pieces_ref[0]
        high = pltpu.roll(pltpu.roll(pieces_ref[1], owner + 1, 0), owner + 1, 1)
        zero = jnp.zeros_like(low)
        low = jnp.where((row <= owner) & (col <= owner), low, zero)
        high = jnp.where((row > owner) & (col > owner) & (col < LEVELS), high, zero)
        top, rest = split((low + high)[:, :LEVELS])
        matrix_ref[...] = jnp.concatenate([top, top, rest], 1)
        moment_ref[...] = jnp.zeros_like(moment_ref)

    base = lax.axis_index("cols") * (col_count // (MEMB * WINDOW))
    total = jnp.zeros((LEVELS, LANES), jnp.float32)
    for line in range(0, lines, 2):
        top, rest = split(
            jnp.concatenate([source[pl.ds(line + i, LEVELS, stride=lines), :] for i in range(2)], 1)
        )
        mixed = jnp.dot(
            matrix_ref[...], jnp.concatenate([top, rest, top], 0), preferred_element_type=jnp.float32
        )
        for i in range(2):
            out = mixed[:, i * LANES : (i + 1) * LANES]
            target[pl.ds(line + i, LEVELS, stride=lines), :] = out
            column = ((step * lines + line + i) * LANES) % col_count
            third = base + column // (MEMB * WINDOW)
            total += (third + 1).astype(jnp.float32) * (out * out)
    moment_ref[...] += jnp.sum(total * (row + 1).astype(jnp.float32), axis=0, keepdims=True)


def turn_kernel(x_ref, cos_ref, sin_ref, out_ref):
    blocks = out_ref.shape[2] // LANES
    lines = 2 * blocks
    flat = x_ref.reshape(LEVELS * lines, LANES)
    n1 = lax.axis_index("pairs")
    tile, shift = n1 // 8, n1 % 8
    back = (8 - shift) % 8

    def rows(part, j):
        turned = []
        for a in range(LEVELS // 8):
            slot = 8 * ((a + tile) % 8)
            turned.append(
                pltpu.roll(flat[pl.ds(slot * lines + part * blocks + j, 8, stride=lines), :], back, 0)
            )
        return [blend(turned[a], turned[(a + 1) % 8], 8 - shift) for a in range(LEVELS // 8)]

    for j in range(blocks):
        lanes = slice(j * LANES, (j + 1) * LANES)
        real, imag = rows(0, j), rows(1, j)
        for a in range(LEVELS // 8):
            span = slice(8 * a, 8 * a + 8)
            cosine, sine = cos_ref[span, lanes], sin_ref[span, lanes]
            out_ref[0, span, lanes] = cosine * real[a] - sine * imag[a]
            out_ref[1, span, lanes] = sine * real[a] + cosine * imag[a]


def butterfly(value, axis):
    size = lax.axis_size(axis)
    reach = 1
    while reach < size:
        value = value + lax.ppermute(value, axis, [(i, i ^ reach) for i in range(size)])
        reach *= 2
    return value


def local(state, sector_mix, kerr_rates, column_load):
    pair_count = lax.axis_size("pairs")
    col_devices = lax.axis_size("cols")
    device = lax.axis_index("pairs")
    col_device = lax.axis_index("cols")
    levels, col_count = state.shape[2], state.shape[3]
    assert pair_count == levels == LEVELS and state.shape[1] == 1
    state = state.reshape(2, levels, col_count)
    blocks = col_count // LANES
    lines = 2 * blocks
    part = blocks // STEPS
    width = part * LANES
    params = pltpu.CompilerParams(vmem_limit_bytes=VMEM_LIMIT)

    def exchange(rows):
        return lax.all_to_all(rows, "pairs", 0, 0, tiled=True)

    low = lax.dynamic_slice_in_dim(sector_mix, device, 1, 0)
    high = lax.dynamic_slice_in_dim(sector_mix, jnp.minimum(device + levels, 2 * levels - 2), 1, 0)
    mine = jnp.concatenate([low, high], 0)
    share = mine.shape[2]
    pieces = jnp.zeros((2, levels, LANES), jnp.float32)
    for step in range(col_devices):
        ring = [(i, (i + step) % col_devices) for i in range(col_devices)]
        received = lax.ppermute(mine, "cols", ring) if step else mine
        owner = (col_device - step) % col_devices
        pieces = lax.dynamic_update_slice(pieces, received, (0, 0, owner * share))

    rows_spec = pl.BlockSpec((levels, 2, part, LANES), lambda i: (0, 0, i, 0))
    packed = pl.pallas_call(
        pack_kernel,
        grid=(STEPS,),
        in_specs=[pl.BlockSpec((2, levels, width), lambda i: (0, 0, i))],
        out_specs=rows_spec,
        out_shape=pltpu.HBM((levels, 2, blocks, LANES), jnp.float32),
        compiler_params=params,
        name="pack",
    )(pltpu.with_memory_space_constraint(state, pltpu.HBM))
    arrived = exchange(packed.reshape(levels, lines, LANES))

    n1 = device.astype(jnp.float32)
    n2 = jnp.arange(levels).astype(jnp.float32)
    phases = (kerr_rates[0] * n1 + kerr_rates[1] * n2)[:, None] * column_load.astype(jnp.float32)[None, :]
    cosine, sine = jnp.cos(phases), jnp.sin(phases)

    lines_spec = pl.BlockSpec((levels, lines // STEPS, LANES), lambda i: (0, i, 0))
    mixed, moment = pl.pallas_call(
        functools.partial(mix_kernel, col_count),
        grid=(STEPS,),
        in_specs=[lines_spec, pl.BlockSpec((2, levels, LANES), lambda i: (0, 0, 0))],
        out_specs=[lines_spec, pl.BlockSpec((1, LANES), lambda i: (0, 0))],
        out_shape=[
            pltpu.HBM((levels, lines, LANES), jnp.float32),
            jax.ShapeDtypeStruct((1, LANES), jnp.float32),
        ],
        scratch_shapes=[pltpu.VMEM((levels, 3 * levels), jnp.bfloat16)],
        compiler_params=params,
        name="mix",
    )(arrived, pieces)
    returned = exchange(mixed).reshape(levels, 2, blocks, LANES)

    summed = jnp.sum(butterfly(butterfly(moment, "cols"), "pairs"))
    moment = summed / float(levels * levels * col_count * col_devices * levels * THIRD)

    table = pl.BlockSpec((levels, width), lambda i: (0, i))
    evolved = pl.pallas_call(
        turn_kernel,
        grid=(STEPS,),
        in_specs=[rows_spec, table, table],
        out_specs=pl.BlockSpec((2, levels, width), lambda i: (0, 0, i)),
        out_shape=jax.ShapeDtypeStruct((2, levels, col_count), jnp.float32),
        compiler_params=params,
        name="turn",
    )(returned, cosine, sine)
    return evolved.reshape(2, 1, levels, col_count), moment.reshape(1)


def solution(mesh):
    placed = (P(None, "pairs", None, "cols"), P(None, None, "cols"), P(), P("cols"))
    return jax.shard_map(
        local,
        mesh=mesh,
        in_specs=placed,
        out_specs=(P(None, "pairs", None, "cols"), P()),
        check_vma=False,
    )
```

time: 216 us -> 145 us (0.67)
  blocking collectives: 78.3 us -> 0 us
  waiting for transfers between devices: 62.4 us -> 76.6 us
  Pallas kernels: 21.2 us -> 9.88 us
  starting transfers between devices: 36.8 us -> 41.5 us
    psum x1 -> x0, blocking collectives: 78.3 us -> none  [local(): summed = lax.psum(jnp.sum(sum(moments)), ('pairs', 'cols'))]
    ppermute x3 -> x11, waiting for transfers between devices: 1.05 us -> 37.7 us  [the longest x8 36.7 us: butterfly(): lax.ppermute(value, axis, [(i, i ^ reach) for i in range(size)])]
    all_to_all x4 -> x2, waiting for transfers between devices: 61.4 us -> 38.9 us  [exchange(): return lax.all_to_all(rows, 'pairs', 0, 0, tiled=True)]
    ppermute x3 -> x11, starting transfers between devices: 4.85 us -> 21.2 us  [the longest x8 16.3 us: butterfly(): lax.ppermute(value, axis, [(i, i ^ reach) for i in range(size)])]
    all_to_all x4 -> x2, starting transfers between devices: 32 us -> 20.4 us  [exchange(): return lax.all_to_all(rows, 'pairs', 0, 0, tiled=True)]
    pallas_call x6 -> x3, Pallas kernels: 21.2 us -> 9.88 us  [the longest x1 4.27 us: local(): pl.pallas_call(pack_kernel, grid=(STEPS,), in_specs=[pl.BlockSpec((2, lev...]
  transfers between devices with their start and end apart: 7 -> 13, of which waited for: 4 -> 9; matrix products, arithmetic and copies ran while one was open for 5% -> 8% of each run, Pallas kernels for 7% -> 0%
where the time goes in v2:
time: 145 us; the launch traced here: 144 us
  waiting for transfers between devices  76.6 us (53%)
  starting transfers between devices  41.5 us (29%)
  Pallas kernels  9.88 us (7%)
  local copies, waits for them, and re-layouts  6.68 us (5%)
  other arithmetic  5.89 us (4%)
  between operations  3.22 us (2%)
    all_to_all x2, waiting for transfers between devices, exchange(): return lax.all_to_all(rows, 'pairs', 0, 0, tiled=True)  38.9 us
    ppermute x8, waiting for transfers between devices, butterfly(): lax.ppermute(value, axis, [(i, i ^ reach) for i in range(size)])  36.7 us
    all_to_all x2, starting transfers between devices, exchange(): return lax.all_to_all(rows, 'pairs', 0, 0, tiled=True)  20.4 us
    ppermute x8, starting transfers between devices, butterfly(): lax.ppermute(value, axis, [(i, i ^ reach) for i in range(size)])  16.3 us
    ppermute x3, starting transfers between devices, local(): received = lax.ppermute(mine, 'cols', ring) if step else mine  4.85 us
    sin x1, other arithmetic, local(): cosine, sine = (jnp.cos(phases), jnp.sin(phases))  4.69 us
    pallas_call x1, Pallas kernels, local(): pl.pallas_call(pack_kernel, grid=(STEPS,), in_specs=[pl.BlockSpec((2, lev...  4.27 us
    pallas_call x1, Pallas kernels, local(): pl.pallas_call(functools.partial(mix_kernel, col_count), grid=(STEPS,), i...  3.06 us
  transfers between devices with their start and end apart: 13, of which 9 were waited for; matrix products, arithmetic and copies ran while one was open for 8% of the time, Pallas kernels for 0%

profile of v2, /device:TPU:1, one launch (start us, length us, event | category | flops | bytes accessed | tf_op | source)
XLA Modules:
  0.0 143.8 jit_solution(15720881619407462739)
XLA Ops:
  0.6 4.3 %pack.1 = f32[64,2,32,128]{3,2,1,0:T(8,128)} custom-call(f32[2,64,4096]{2,1,0:T(8,128)} %bitcast.12), custom_call_target="tpu_custom_call" | custom-call | tf_op jit(solution)/shard_map/pack/pallas_call | solution.py:151
  4.9 0.0 copy-start.1
  4.9 13.3 %all-to-all-start = ((f32[64,64,128]{2,1,0:T(8,128)}), f32[64,64,128]{2,1,0:T(8,128)S(1)}, u32[]{:S(2)}, u32[]{:S(2)}) async-start(f32[64,64,128]{2,1,0:T(8,128)} %bitcast.10), calls=%async_computation | async-start | bytes 4194304 | tf_op jit(solution)/shard_map/all_to_all | solution.py:137
  18.2 0.0 copy-done.1
  18.2 1.1 constant_dynamic-slice_fusion.1
  19.3 1.3 copy.16
  20.6 0.3 copy.17
  20.9 0.1 copy.11
  21.0 1.2 collective-permute-start
  22.2 2.5 %collective-permute-start.1 = (f32[2,64,16]{2,1,0:T(8,128)S(1)}, f32[2,64,16]{2,1,0:T(8,128)S(1)}, u32[]{:S(2)}, u32[]{:S(2)}) collective-permute-start(f32[2,64,16]{2,1,0:T(8,128)S(1)} %copy.11), channel_id=1, source_target_pairs={{0,2},{1,3},{2,0},{3,1},{4,6},{5,7},{6,4},{7,5},{8,10},{9,11},{10,... | collective-permute-start | bytes 24584 | tf_op jit(solution)/shard_map/ppermute | solution.py:146
  24.7 1.2 collective-permute-start.2
  25.8 0.3 dynamic_update_slice.12
  26.1 0.0 collective-permute-done
  26.1 0.6 dynamic_update_slice.13
  26.8 1.0 collective-permute-done.1
  27.8 0.6 dynamic_update_slice.14
  28.4 0.0 collective-permute-done.2
  28.4 0.6 dynamic_update_slice.15.pieces_ref
  29.0 38.9 %all-to-all-done.x_ref = f32[64,64,128]{2,1,0:T(8,128)S(1)} async-done(((f32[64,64,128]{2,1,0:T(8,128)}), f32[64,64,128]{2,1,0:T(8,128)S(1)}, u32[]{:S(2)}, u32[]{:S(2)}) %all-to-all-start) | async-done | bytes 2097184 | tf_op jit(solution)/shard_map/all_to_all | solution.py:137
  67.9 3.1 %mix.1 = (f32[64,64,128]{2,1,0:T(8,128)}, f32[1,128]{1,0:T(1,128)S(1)}) custom-call(f32[64,64,128]{2,1,0:T(8,128)S(1)} %all-to-all-done.x_ref, f32[2,64,128]{2,1,0:T(8,128)S(1)} %dynamic_update_slice.15.pieces_ref), custom_call_target="tpu_custom_call" | custom-call | tf_op jit(solution)/shard_map/mix/pallas_call | solution.py:168
  70.9 0.0 copy-start.3
  71.0 7.1 %all-to-all-start.1 = ((f32[64,64,128]{2,1,0:T(8,128)}), f32[64,64,128]{2,1,0:T(8,128)S(1)}, u32[]{:S(2)}, u32[]{:S(2)}) async-start(f32[64,64,128]{2,1,0:T(8,128)} %get-tuple-element.4), calls=%async_computation.1 | async-start | bytes 4194304 | tf_op jit(solution)/shard_map/all_to_all | solution.py:137
  78.1 1.3 collective-permute-start.3
  79.4 1.5 %collective-permute-done.3 = f32[1,128]{1,0:T(1,128)S(1)} collective-permute-done((f32[1,128]{1,0:T(1,128)S(1)}, f32[1,128]{1,0:T(1,128)S(1)}, u32[]{:S(2)}, u32[]{:S(2)}) %collective-permute-start.3) | collective-permute-done | bytes 544 | tf_op jit(solution)/shard_map/ppermute | solution.py:117
  80.9 2.7 %collective-permute-start.4 = (f32[1,128]{1,0:T(1,128)S(1)}, f32[1,128]{1,0:T(1,128)S(1)}, u32[]{:S(2)}, u32[]{:S(2)}) collective-permute-start(f32[1,128]{1,0:T(1,128)S(1)} %add.84), channel_id=1, source_target_pairs={{0,2},{1,3},{2,0},{3,1},{4,6},{5,7},{6,4},{7,5},{8,10},{9,11},{10,... | collective-permute-start | bytes 1544 | tf_op jit(solution)/shard_map/ppermute | solution.py:117
  83.6 1.5 %collective-permute-done.4 = f32[1,128]{1,0:T(1,128)S(1)} collective-permute-done((f32[1,128]{1,0:T(1,128)S(1)}, f32[1,128]{1,0:T(1,128)S(1)}, u32[]{:S(2)}, u32[]{:S(2)}) %collective-permute-start.4) | collective-permute-done | bytes 544 | tf_op jit(solution)/shard_map/ppermute | solution.py:117
  85.1 2.2 %collective-permute-start.5 = (f32[1,128]{1,0:T(1,128)S(1)}, f32[1,128]{1,0:T(1,128)S(1)}, u32[]{:S(2)}, u32[]{:S(2)}) collective-permute-start(f32[1,128]{1,0:T(1,128)S(1)} %add.85), channel_id=1, source_target_pairs={{0,4},{4,0},{8,12},{12,8},{16,20},{20,16},{24,28},{28,24},{32,36},... | collective-permute-start | bytes 1544 | tf_op jit(solution)/shard_map/ppermute | solution.py:117
  87.2 0.8 collective-permute-done.5
  88.1 1.3 collective-permute-start.6
  89.4 1.4 collective-permute-done.6
  90.8 2.9 %collective-permute-start.7 = (f32[1,128]{1,0:T(1,128)S(1)}, f32[1,128]{1,0:T(1,128)S(1)}, u32[]{:S(2)}, u32[]{:S(2)}) collective-permute-start(f32[1,128]{1,0:T(1,128)S(1)} %add.87), channel_id=1, source_target_pairs={{0,16},{4,20},{8,24},{12,28},{16,0},{20,4},{24,8},{28,12},{32,48},... | collective-permute-start | bytes 1544 | tf_op jit(solution)/shard_map/ppermute | solution.py:117
  93.6 1.4 collective-permute-done.7
  95.0 1.3 collective-permute-start.8
  96.3 0.0 copy-done.3
  96.3 0.6 fusion
  97.6 27.1 %collective-permute-done.8 = f32[1,128]{1,0:T(1,128)S(1)} collective-permute-done((f32[1,128]{1,0:T(1,128)S(1)}, f32[1,128]{1,0:T(1,128)S(1)}, u32[]{:S(2)}, u32[]{:S(2)}) %collective-permute-start.8) | collective-permute-done | bytes 544 | tf_op jit(solution)/shard_map/ppermute | solution.py:117
  124.6 0.0 collective-permute-start.9
  124.6 0.6 multiply_add_fusion
  125.2 0.0 copy-done.2
  125.2 3.0 %collective-permute-done.9 = f32[1,128]{1,0:T(1,128)S(1)} collective-permute-done((f32[1,128]{1,0:T(1,128)S(1)}, f32[1,128]{1,0:T(1,128)S(1)}, u32[]{:S(2)}, u32[]{:S(2)}) %collective-permute-start.9) | collective-permute-done | bytes 544 | tf_op jit(solution)/shard_map/ppermute | solution.py:117
  128.3 4.7 %collective-permute-start.10 = (f32[1,128]{1,0:T(1,128)S(1)}, f32[1,128]{1,0:T(1,128)S(1)}, u32[]{:S(2)}, u32[]{:S(2)}) collective-permute-start(f32[1,128]{1,0:T(1,128)S(1)} %add.90), channel_id=1, source_target_pairs={{0,128},{4,132},{8,136},{12,140},{16,144},{20,148},{24,152},{28,15... | collective-permute-start | bytes 1544 | tf_op jit(solution)/shard_map/ppermute | solution.py:117
  132.9 4.7 %multiply_sine_fusion = (f32[64,4096]{1,0:T(8,128)S(1)}, f32[64,4096]{1,0:T(8,128)}) fusion(f32[4096]{0:T(1024)S(1)} %convert_element_type.15, f32[64]{0:T(128)S(1)} %multiply_add_fusion), kind=kLoop, calls=%fused_computation | loop fusion | flops 262144 | bytes 2113792 | tf_op jit(solution)/shard_map/sin | solution.py:165
  137.6 0.0 collective-permute-done.10
  137.6 0.6 add_reduce_fusion
  138.9 0.0 all-to-all-done.1
  138.9 0.0 copy-start
  138.9 1.2 copy-done
  140.1 2.6 %turn.1 = f32[2,64,4096]{2,1,0:T(8,128)} custom-call(f32[64,2,32,128]{3,2,1,0:T(8,128)S(1)} %bitcast.9, f32[64,4096]{1,0:T(8,128)S(1)} %copy-done, f32[64,4096]{1,0:T(8,128)S(1)} %get-tuple-element.12.sin_ref), custom_call_target="tpu_custom_call" | custom-call | tf_op jit(solution)/shard_map/turn/pallas_call | solution.py:187
  (11 shorter events, 0.0 us)
Async XLA Ops:
  4.9 13.3 %copy-start.1 = (f32[127,64,16]{0,2,1:T(8,128)S(1)}, f32[127,64,16]{0,2,1:T(8,128)}, u32[]{:S(2)}) copy-start(f32[127,64,16]{0,2,1:T(8,128)} %param.5) | copy-start | bytes 1560580
  4.9 63.0 %all-to-all-start = ((f32[64,64,128]{2,1,0:T(8,128)}), f32[64,64,128]{2,1,0:T(8,128)S(1)}, u32[]{:S(2)}, u32[]{:S(2)}) async-start(f32[64,64,128]{2,1,0:T(8,128)} %bitcast.10), calls=%async_computation | async-start | bytes 4194304 | tf_op jit(solution)/shard_map/all_to_all | solution.py:137
  21.0 5.2 %collective-permute-start = (f32[2,64,16]{2,1,0:T(8,128)S(1)}, f32[2,64,16]{2,1,0:T(8,128)S(1)}, u32[]{:S(2)}, u32[]{:S(2)}) collective-permute-start(f32[2,64,16]{2,1,0:T(8,128)S(1)} %copy.11), channel_id=1, source_target_pairs={{0,1},{1,2},{2,3},{3,0},{4,5},{5,6},{6,7},{7,4},{8,9},{9,10},{10,1... | collective-permute-start | bytes 24584 | tf_op jit(solution)/shard_map/ppermute | solution.py:146
  22.2 5.6 %collective-permute-start.1 = (f32[2,64,16]{2,1,0:T(8,128)S(1)}, f32[2,64,16]{2,1,0:T(8,128)S(1)}, u32[]{:S(2)}, u32[]{:S(2)}) collective-permute-start(f32[2,64,16]{2,1,0:T(8,128)S(1)} %copy.11), channel_id=1, source_target_pairs={{0,2},{1,3},{2,0},{3,1},{4,6},{5,7},{6,4},{7,5},{8,10},{9,11},{10,... | collective-permute-start | bytes 24584 | tf_op jit(solution)/shard_map/ppermute | solution.py:146
  24.7 3.7 %collective-permute-start.2 = (f32[2,64,16]{2,1,0:T(8,128)S(1)}, f32[2,64,16]{2,1,0:T(8,128)S(1)}, u32[]{:S(2)}, u32[]{:S(2)}) collective-permute-start(f32[2,64,16]{2,1,0:T(8,128)S(1)} %copy.11), channel_id=1, source_target_pairs={{0,3},{1,0},{2,1},{3,2},{4,7},{5,4},{6,5},{7,6},{8,11},{9,8},{10,9... | collective-permute-start | bytes 24584 | tf_op jit(solution)/shard_map/ppermute | solution.py:146
  70.9 25.4 %copy-start.3 = (f32[2]{0:T(128)S(1)}, f32[2]{0:T(128)}, u32[]{:S(2)}) copy-start(f32[2]{0:T(128)} %param.6) | copy-start | bytes 28
  71.0 54.3 %copy-start.2 = (s32[4096]{0:T(1024)S(1)}, s32[4096]{0:T(1024)}, u32[]{:S(2)}) copy-start(s32[4096]{0:T(1024)} %param.7) | copy-start | bytes 49156
  71.0 67.9 %all-to-all-start.1 = ((f32[64,64,128]{2,1,0:T(8,128)}), f32[64,64,128]{2,1,0:T(8,128)S(1)}, u32[]{:S(2)}, u32[]{:S(2)}) async-start(f32[64,64,128]{2,1,0:T(8,128)} %get-tuple-element.4), calls=%async_computation.1 | async-start | bytes 4194304 | tf_op jit(solution)/shard_map/all_to_all | solution.py:137
  78.1 2.8 %collective-permute-start.3 = (f32[1,128]{1,0:T(1,128)S(1)}, f32[1,128]{1,0:T(1,128)S(1)}, u32[]{:S(2)}, u32[]{:S(2)}) collective-permute-start(f32[1,128]{1,0:T(1,128)S(1)} %get-tuple-element.5), channel_id=1, source_target_pairs={{0,1},{1,0},{2,3},{3,2},{4,5},{5,4},{6,7},{7,6},{8,9},{9,8},{10,11... | collective-permute-start | bytes 1544 | tf_op jit(solution)/shard_map/ppermute | solution.py:117
  80.9 4.2 %collective-permute-start.4 = (f32[1,128]{1,0:T(1,128)S(1)}, f32[1,128]{1,0:T(1,128)S(1)}, u32[]{:S(2)}, u32[]{:S(2)}) collective-permute-start(f32[1,128]{1,0:T(1,128)S(1)} %add.84), channel_id=1, source_target_pairs={{0,2},{1,3},{2,0},{3,1},{4,6},{5,7},{6,4},{7,5},{8,10},{9,11},{10,... | collective-permute-start | bytes 1544 | tf_op jit(solution)/shard_map/ppermute | solution.py:117
  85.1 3.0 %collective-permute-start.5 = (f32[1,128]{1,0:T(1,128)S(1)}, f32[1,128]{1,0:T(1,128)S(1)}, u32[]{:S(2)}, u32[]{:S(2)}) collective-permute-start(f32[1,128]{1,0:T(1,128)S(1)} %add.85), channel_id=1, source_target_pairs={{0,4},{4,0},{8,12},{12,8},{16,20},{20,16},{24,28},{28,24},{32,36},... | collective-permute-start | bytes 1544 | tf_op jit(solution)/shard_map/ppermute | solution.py:117
  88.1 2.7 %collective-permute-start.6 = (f32[1,128]{1,0:T(1,128)S(1)}, f32[1,128]{1,0:T(1,128)S(1)}, u32[]{:S(2)}, u32[]{:S(2)}) collective-permute-start(f32[1,128]{1,0:T(1,128)S(1)} %add.86), channel_id=1, source_target_pairs={{0,8},{4,12},{8,0},{12,4},{16,24},{20,28},{24,16},{28,20},{32,40},... | collective-permute-start | bytes 1544 | tf_op jit(solution)/shard_map/ppermute | solution.py:117
  90.8 4.2 %collective-permute-start.7 = (f32[1,128]{1,0:T(1,128)S(1)}, f32[1,128]{1,0:T(1,128)S(1)}, u32[]{:S(2)}, u32[]{:S(2)}) collective-permute-start(f32[1,128]{1,0:T(1,128)S(1)} %add.87), channel_id=1, source_target_pairs={{0,16},{4,20},{8,24},{12,28},{16,0},{20,4},{24,8},{28,12},{32,48},... | collective-permute-start | bytes 1544 | tf_op jit(solution)/shard_map/ppermute | solution.py:117
  95.0 29.6 %collective-permute-start.8 = (f32[1,128]{1,0:T(1,128)S(1)}, f32[1,128]{1,0:T(1,128)S(1)}, u32[]{:S(2)}, u32[]{:S(2)}) collective-permute-start(f32[1,128]{1,0:T(1,128)S(1)} %add.88), channel_id=1, source_target_pairs={{0,32},{4,36},{8,40},{12,44},{16,48},{20,52},{24,56},{28,60},{32,0... | collective-permute-start | bytes 1544 | tf_op jit(solution)/shard_map/ppermute | solution.py:117
  124.6 3.6 %collective-permute-start.9 = (f32[1,128]{1,0:T(1,128)S(1)}, f32[1,128]{1,0:T(1,128)S(1)}, u32[]{:S(2)}, u32[]{:S(2)}) collective-permute-start(f32[1,128]{1,0:T(1,128)S(1)} %add.89), channel_id=1, source_target_pairs={{0,64},{4,68},{8,72},{12,76},{16,80},{20,84},{24,88},{28,92},{32,9... | collective-permute-start | bytes 1544 | tf_op jit(solution)/shard_map/ppermute | solution.py:117
  128.3 9.4 %collective-permute-start.10 = (f32[1,128]{1,0:T(1,128)S(1)}, f32[1,128]{1,0:T(1,128)S(1)}, u32[]{:S(2)}, u32[]{:S(2)}) collective-permute-start(f32[1,128]{1,0:T(1,128)S(1)} %add.90), channel_id=1, source_target_pairs={{0,128},{4,132},{8,136},{12,140},{16,144},{20,148},{24,152},{28,15... | collective-permute-start | bytes 1544 | tf_op jit(solution)/shard_map/ppermute | solution.py:117
  138.9 1.2 copy-start

commit v3 on v2

--- a/solution.py
+++ b/solution.py
@@ -77,7 +77,7 @@
         for i in range(2):
             out = mixed[:, i * LANES : (i + 1) * LANES]
             target[pl.ds(line + i, LEVELS, stride=lines), :] = out
-            column = ((step * lines + line + i) * LANES) % col_count
+            column = (step * (lines // 2) + (line + i) % (lines // 2)) * LANES
             third = base + column // (MEMB * WINDOW)
             total += (third + 1).astype(jnp.float32) * (out * out)
     moment_ref[...] += jnp.sum(total * (row + 1).astype(jnp.float32), axis=0, keepdims=True)
@@ -147,29 +147,29 @@
         owner = (col_device - step) % col_devices
         pieces = lax.dynamic_update_slice(pieces, received, (0, 0, owner * share))
 
-    rows_spec = pl.BlockSpec((levels, 2, part, LANES), lambda i: (0, 0, i, 0))
+    rows_spec = pl.BlockSpec((levels, 2 * part, LANES), lambda i: (0, i, 0))
     packed = pl.pallas_call(
         pack_kernel,
         grid=(STEPS,),
         in_specs=[pl.BlockSpec((2, levels, width), lambda i: (0, 0, i))],
         out_specs=rows_spec,
-        out_shape=pltpu.HBM((levels, 2, blocks, LANES), jnp.float32),
+        out_shape=pltpu.HBM((levels, lines, LANES), jnp.float32),
         compiler_params=params,
         name="pack",
     )(pltpu.with_memory_space_constraint(state, pltpu.HBM))
-    arrived = exchange(packed.reshape(levels, lines, LANES))
+    arrived = exchange(packed)
 
     n1 = device.astype(jnp.float32)
     n2 = jnp.arange(levels).astype(jnp.float32)
     phases = (kerr_rates[0] * n1 + kerr_rates[1] * n2)[:, None] * column_load.astype(jnp.float32)[None, :]
     cosine, sine = jnp.cos(phases), jnp.sin(phases)
 
-    lines_spec = pl.BlockSpec((levels, lines // STEPS, LANES), lambda i: (0, i, 0))
+    arrived, cosine, sine = lax.optimization_barrier((arrived, cosine, sine))
     mixed, moment = pl.pallas_call(
         functools.partial(mix_kernel, col_count),
         grid=(STEPS,),
-        in_specs=[lines_spec, pl.BlockSpec((2, levels, LANES), lambda i: (0, 0, 0))],
-        out_specs=[lines_spec, pl.BlockSpec((1, LANES), lambda i: (0, 0))],
+        in_specs=[rows_spec, pl.BlockSpec((2, levels, LANES), lambda i: (0, 0, 0))],
+        out_specs=[rows_spec, pl.BlockSpec((1, LANES), lambda i: (0, 0))],
         out_shape=[
             pltpu.HBM((levels, lines, LANES), jnp.float32),
             jax.ShapeDtypeStruct((1, LANES), jnp.float32),
@@ -178,7 +178,7 @@
         compiler_params=params,
         name="mix",
     )(arrived, pieces)
-    returned = exchange(mixed).reshape(levels, 2, blocks, LANES)
+    returned = exchange(mixed)
 
     summed = jnp.sum(butterfly(butterfly(moment, "cols"), "pairs"))
     moment = summed / float(levels * levels * col_count * col_devices * levels * THIRD)
@@ -192,7 +192,7 @@
         out_shape=jax.ShapeDtypeStruct((2, levels, col_count), jnp.float32),
         compiler_params=params,
         name="turn",
-    )(returned, cosine, sine)
+    )(returned, *(pltpu.with_memory_space_constraint(t, pltpu.HBM) for t in (cosine, sine)))
     return evolved.reshape(2, 1, levels, col_count), moment.reshape(1)
 
 

time: 145 us -> 143 us (0.986)
  waiting for transfers between devices: 76.6 us -> 73.1 us
  Pallas kernels: 9.88 us -> 11.4 us
    all_to_all x2, waiting for transfers between devices: 38.9 us -> 33 us  [exchange(): return lax.all_to_all(rows, 'pairs', 0, 0, tiled=True)]
    ppermute x8, waiting for transfers between devices: 36.7 us -> 40.2 us  [butterfly(): lax.ppermute(value, axis, [(i, i ^ reach) for i in range(size)])]
    pallas_call x1, Pallas kernels: 2.55 us -> 4.15 us  [local(): pl.pallas_call(turn_kernel, grid=(STEPS,), in_specs=[rows_spec, table, ta...]
where the time goes in v3:
time: 143 us; the launch traced here: 141 us
  waiting for transfers between devices  73.1 us (51%)
  starting transfers between devices  41.4 us (29%)
  Pallas kernels  11.4 us (8%)
  other arithmetic  6.14 us (4%)
  local copies, waits for them, and re-layouts  5.6 us (4%)
  between operations  3.22 us (2%)
    ppermute x8, waiting for transfers between devices, butterfly(): lax.ppermute(value, axis, [(i, i ^ reach) for i in range(size)])  40.2 us
    all_to_all x2, waiting for transfers between devices, exchange(): return lax.all_to_all(rows, 'pairs', 0, 0, tiled=True)  33 us
    all_to_all x2, starting transfers between devices, exchange(): return lax.all_to_all(rows, 'pairs', 0, 0, tiled=True)  20.2 us
    ppermute x8, starting transfers between devices, butterfly(): lax.ppermute(value, axis, [(i, i ^ reach) for i in range(size)])  16.3 us
    ppermute x3, starting transfers between devices, local(): received = lax.ppermute(mine, 'cols', ring) if step else mine  4.85 us
    sin x1, other arithmetic, local(): cosine, sine = (jnp.cos(phases), jnp.sin(phases))  4.81 us
    pallas_call x1, Pallas kernels, local(): pl.pallas_call(pack_kernel, grid=(STEPS,), in_specs=[pl.BlockSpec((2, lev...  4.27 us
    pallas_call x1, Pallas kernels, local(): pl.pallas_call(turn_kernel, grid=(STEPS,), in_specs=[rows_spec, table, ta...  4.15 us
  transfers between devices with their start and end apart: 13, of which 9 were waited for; matrix products, arithmetic and copies ran while one was open for 8% of the time, Pallas kernels for 0%

profile of v3, /device:TPU:1, one launch (start us, length us, event | category | flops | bytes accessed | tf_op | source)
XLA Modules:
  0.0 140.9 jit_solution(3411469960528924035)
XLA Ops:
  0.6 4.3 %pack.1 = f32[64,64,128]{2,1,0:T(8,128)} custom-call(f32[2,64,4096]{2,1,0:T(8,128)} %bitcast.8), custom_call_target="tpu_custom_call" | custom-call | tf_op jit(solution)/shard_map/pack/pallas_call | solution.py:151
  4.9 0.0 copy-start
  4.9 13.3 %all-to-all-start = ((f32[64,64,128]{2,1,0:T(8,128)}), f32[64,64,128]{2,1,0:T(8,128)S(1)}, u32[]{:S(2)}, u32[]{:S(2)}) async-start(f32[64,64,128]{2,1,0:T(8,128)} %pack.1), calls=%async_computation | async-start | bytes 4194304 | tf_op jit(solution)/shard_map/all_to_all | solution.py:137
  18.2 0.0 copy-start.1
  18.2 0.0 copy-start.2
  18.2 0.0 copy-done
  18.2 1.1 constant_dynamic-slice_fusion.1
  19.4 1.3 copy.17
  20.6 0.3 copy.16
  20.9 0.1 copy.11
  21.0 1.2 collective-permute-start
  22.2 2.5 %collective-permute-start.1 = (f32[2,64,16]{2,1,0:T(8,128)S(1)}, f32[2,64,16]{2,1,0:T(8,128)S(1)}, u32[]{:S(2)}, u32[]{:S(2)}) collective-permute-start(f32[2,64,16]{2,1,0:T(8,128)S(1)} %copy.11), channel_id=1, source_target_pairs={{0,2},{1,3},{2,0},{3,1},{4,6},{5,7},{6,4},{7,5},{8,10},{9,11},{10,... | collective-permute-start | bytes 24584 | tf_op jit(solution)/shard_map/ppermute | solution.py:146
  24.7 1.2 collective-permute-start.2
  25.9 0.0 copy-done.1
  25.9 0.0 copy-done.2
  25.9 0.7 fusion
  27.2 0.7 multiply_add_fusion
  27.9 4.8 %multiply_sine_fusion = (f32[64,4096]{1,0:T(8,128)}, f32[64,4096]{1,0:T(8,128)}) fusion(f32[4096]{0:T(1024)S(1)} %convert_element_type.15, f32[64]{0:T(128)S(1)} %multiply_add_fusion), kind=kLoop, calls=%fused_computation | loop fusion | flops 262144 | bytes 2113792 | tf_op jit(solution)/shard_map/sin | solution.py:165
  32.7 0.3 dynamic_update_slice.12
  33.0 0.0 collective-permute-done
  33.0 0.6 dynamic_update_slice.13
  33.6 0.0 collective-permute-done.1
  33.7 0.6 dynamic_update_slice.14
  34.3 0.0 collective-permute-done.2
  34.3 0.6 dynamic_update_slice.15.pieces_ref
  34.9 33.0 %all-to-all-done.x_ref = f32[64,64,128]{2,1,0:T(8,128)S(1)} async-done(((f32[64,64,128]{2,1,0:T(8,128)}), f32[64,64,128]{2,1,0:T(8,128)S(1)}, u32[]{:S(2)}, u32[]{:S(2)}) %all-to-all-start) | async-done | bytes 2097184 | tf_op jit(solution)/shard_map/all_to_all | solution.py:137
  67.9 3.0 %mix.1 = (f32[64,64,128]{2,1,0:T(8,128)}, f32[1,128]{1,0:T(1,128)S(1)}) custom-call(f32[64,64,128]{2,1,0:T(8,128)S(1)} %all-to-all-done.x_ref, f32[2,64,128]{2,1,0:T(8,128)S(1)} %dynamic_update_slice.15.pieces_ref), custom_call_target="tpu_custom_call" | custom-call | tf_op jit(solution)/shard_map/mix/pallas_call | solution.py:168
  70.9 7.0 %all-to-all-start.1 = ((f32[64,64,128]{2,1,0:T(8,128)}), f32[64,64,128]{2,1,0:T(8,128)S(1)}, u32[]{:S(2)}, u32[]{:S(2)}) async-start(f32[64,64,128]{2,1,0:T(8,128)} %get-tuple-element.8), calls=%async_computation.1 | async-start | bytes 4194304 | tf_op jit(solution)/shard_map/all_to_all | solution.py:137
  77.8 1.3 collective-permute-start.3
  79.1 1.5 %collective-permute-done.3 = f32[1,128]{1,0:T(1,128)S(1)} collective-permute-done((f32[1,128]{1,0:T(1,128)S(1)}, f32[1,128]{1,0:T(1,128)S(1)}, u32[]{:S(2)}, u32[]{:S(2)}) %collective-permute-start.3) | collective-permute-done | bytes 544 | tf_op jit(solution)/shard_map/ppermute | solution.py:117
  80.7 2.7 %collective-permute-start.4 = (f32[1,128]{1,0:T(1,128)S(1)}, f32[1,128]{1,0:T(1,128)S(1)}, u32[]{:S(2)}, u32[]{:S(2)}) collective-permute-start(f32[1,128]{1,0:T(1,128)S(1)} %add.84), channel_id=1, source_target_pairs={{0,2},{1,3},{2,0},{3,1},{4,6},{5,7},{6,4},{7,5},{8,10},{9,11},{10,... | collective-permute-start | bytes 1544 | tf_op jit(solution)/shard_map/ppermute | solution.py:117
  83.4 1.5 %collective-permute-done.4 = f32[1,128]{1,0:T(1,128)S(1)} collective-permute-done((f32[1,128]{1,0:T(1,128)S(1)}, f32[1,128]{1,0:T(1,128)S(1)}, u32[]{:S(2)}, u32[]{:S(2)}) %collective-permute-start.4) | collective-permute-done | bytes 544 | tf_op jit(solution)/shard_map/ppermute | solution.py:117
  84.9 2.2 %collective-permute-start.5 = (f32[1,128]{1,0:T(1,128)S(1)}, f32[1,128]{1,0:T(1,128)S(1)}, u32[]{:S(2)}, u32[]{:S(2)}) collective-permute-start(f32[1,128]{1,0:T(1,128)S(1)} %add.85), channel_id=1, source_target_pairs={{0,4},{4,0},{8,12},{12,8},{16,20},{20,16},{24,28},{28,24},{32,36},... | collective-permute-start | bytes 1544 | tf_op jit(solution)/shard_map/ppermute | solution.py:117
  87.0 0.8 collective-permute-done.5
  87.9 1.3 collective-permute-start.6
  89.2 1.4 %collective-permute-done.6 = f32[1,128]{1,0:T(1,128)S(1)} collective-permute-done((f32[1,128]{1,0:T(1,128)S(1)}, f32[1,128]{1,0:T(1,128)S(1)}, u32[]{:S(2)}, u32[]{:S(2)}) %collective-permute-start.6) | collective-permute-done | bytes 544 | tf_op jit(solution)/shard_map/ppermute | solution.py:117
  90.6 2.9 %collective-permute-start.7 = (f32[1,128]{1,0:T(1,128)S(1)}, f32[1,128]{1,0:T(1,128)S(1)}, u32[]{:S(2)}, u32[]{:S(2)}) collective-permute-start(f32[1,128]{1,0:T(1,128)S(1)} %add.87), channel_id=1, source_target_pairs={{0,16},{4,20},{8,24},{12,28},{16,0},{20,4},{24,8},{28,12},{32,48},... | collective-permute-start | bytes 1544 | tf_op jit(solution)/shard_map/ppermute | solution.py:117
  93.4 1.4 collective-permute-done.7
  94.8 1.3 collective-permute-start.8
  96.1 28.3 %collective-permute-done.8 = f32[1,128]{1,0:T(1,128)S(1)} collective-permute-done((f32[1,128]{1,0:T(1,128)S(1)}, f32[1,128]{1,0:T(1,128)S(1)}, u32[]{:S(2)}, u32[]{:S(2)}) %collective-permute-start.8) | collective-permute-done | bytes 544 | tf_op jit(solution)/shard_map/ppermute | solution.py:117
  124.4 0.0 collective-permute-start.9
  124.4 3.6 %collective-permute-done.9 = f32[1,128]{1,0:T(1,128)S(1)} collective-permute-done((f32[1,128]{1,0:T(1,128)S(1)}, f32[1,128]{1,0:T(1,128)S(1)}, u32[]{:S(2)}, u32[]{:S(2)}) %collective-permute-start.9) | collective-permute-done | bytes 544 | tf_op jit(solution)/shard_map/ppermute | solution.py:117
  128.1 4.7 %collective-permute-start.10 = (f32[1,128]{1,0:T(1,128)S(1)}, f32[1,128]{1,0:T(1,128)S(1)}, u32[]{:S(2)}, u32[]{:S(2)}) collective-permute-start(f32[1,128]{1,0:T(1,128)S(1)} %add.90), channel_id=1, source_target_pairs={{0,128},{4,132},{8,136},{12,140},{16,144},{20,148},{24,152},{28,15... | collective-permute-start | bytes 1544 | tf_op jit(solution)/shard_map/ppermute | solution.py:117
  132.7 1.7 %collective-permute-done.10 = f32[1,128]{1,0:T(1,128)S(1)} collective-permute-done((f32[1,128]{1,0:T(1,128)S(1)}, f32[1,128]{1,0:T(1,128)S(1)}, u32[]{:S(2)}, u32[]{:S(2)}) %collective-permute-start.10) | collective-permute-done | bytes 544 | tf_op jit(solution)/shard_map/ppermute | solution.py:117
  134.4 0.6 add_reduce_fusion
  135.6 0.0 all-to-all-done.1.x_ref
  135.6 4.1 %turn.1 = f32[2,64,4096]{2,1,0:T(8,128)} custom-call(f32[64,64,128]{2,1,0:T(8,128)S(1)} %all-to-all-done.1.x_ref, f32[64,4096]{1,0:T(8,128)} %get-tuple-element.9.cos_ref, f32[64,4096]{1,0:T(8,128)} %get-tuple-element.10.sin_ref), custom_call_target="tpu_custom_call" | custom-call | tf_op jit(solution)/shard_map/turn/pallas_call | solution.py:187
  (10 shorter events, 0.0 us)
Async XLA Ops:
  4.9 13.3 %copy-start = (f32[127,64,16]{0,2,1:T(8,128)S(1)}, f32[127,64,16]{0,2,1:T(8,128)}, u32[]{:S(2)}) copy-start(f32[127,64,16]{0,2,1:T(8,128)} %param.5) | copy-start | bytes 1560580
  4.9 63.0 %all-to-all-start = ((f32[64,64,128]{2,1,0:T(8,128)}), f32[64,64,128]{2,1,0:T(8,128)S(1)}, u32[]{:S(2)}, u32[]{:S(2)}) async-start(f32[64,64,128]{2,1,0:T(8,128)} %pack.1), calls=%async_computation | async-start | bytes 4194304 | tf_op jit(solution)/shard_map/all_to_all | solution.py:137
  18.2 7.7 %copy-start.1 = (s32[4096]{0:T(1024)S(1)}, s32[4096]{0:T(1024)}, u32[]{:S(2)}) copy-start(s32[4096]{0:T(1024)} %param.7) | copy-start | bytes 49156
  18.2 7.7 %copy-start.2 = (f32[2]{0:T(128)S(1)}, f32[2]{0:T(128)}, u32[]{:S(2)}) copy-start(f32[2]{0:T(128)} %param.6) | copy-start | bytes 28
  21.0 12.0 %collective-permute-start = (f32[2,64,16]{2,1,0:T(8,128)S(1)}, f32[2,64,16]{2,1,0:T(8,128)S(1)}, u32[]{:S(2)}, u32[]{:S(2)}) collective-permute-start(f32[2,64,16]{2,1,0:T(8,128)S(1)} %copy.11), channel_id=1, source_target_pairs={{0,1},{1,2},{2,3},{3,0},{4,5},{5,6},{6,7},{7,4},{8,9},{9,10},{10,1... | collective-permute-start | bytes 24584 | tf_op jit(solution)/shard_map/ppermute | solution.py:146
  22.2 11.4 %collective-permute-start.1 = (f32[2,64,16]{2,1,0:T(8,128)S(1)}, f32[2,64,16]{2,1,0:T(8,128)S(1)}, u32[]{:S(2)}, u32[]{:S(2)}) collective-permute-start(f32[2,64,16]{2,1,0:T(8,128)S(1)} %copy.11), channel_id=1, source_target_pairs={{0,2},{1,3},{2,0},{3,1},{4,6},{5,7},{6,4},{7,5},{8,10},{9,11},{10,... | collective-permute-start | bytes 24584 | tf_op jit(solution)/shard_map/ppermute | solution.py:146
  24.7 9.6 %collective-permute-start.2 = (f32[2,64,16]{2,1,0:T(8,128)S(1)}, f32[2,64,16]{2,1,0:T(8,128)S(1)}, u32[]{:S(2)}, u32[]{:S(2)}) collective-permute-start(f32[2,64,16]{2,1,0:T(8,128)S(1)} %copy.11), channel_id=1, source_target_pairs={{0,3},{1,0},{2,1},{3,2},{4,7},{5,4},{6,5},{7,6},{8,11},{9,8},{10,9... | collective-permute-start | bytes 24584 | tf_op jit(solution)/shard_map/ppermute | solution.py:146
  70.9 64.8 %all-to-all-start.1 = ((f32[64,64,128]{2,1,0:T(8,128)}), f32[64,64,128]{2,1,0:T(8,128)S(1)}, u32[]{:S(2)}, u32[]{:S(2)}) async-start(f32[64,64,128]{2,1,0:T(8,128)} %get-tuple-element.8), calls=%async_computation.1 | async-start | bytes 4194304 | tf_op jit(solution)/shard_map/all_to_all | solution.py:137
  77.8 2.8 %collective-permute-start.3 = (f32[1,128]{1,0:T(1,128)S(1)}, f32[1,128]{1,0:T(1,128)S(1)}, u32[]{:S(2)}, u32[]{:S(2)}) collective-permute-start(f32[1,128]{1,0:T(1,128)S(1)} %get-tuple-element.11), channel_id=1, source_target_pairs={{0,1},{1,0},{2,3},{3,2},{4,5},{5,4},{6,7},{7,6},{8,9},{9,8},{10,11... | collective-permute-start | bytes 1544 | tf_op jit(solution)/shard_map/ppermute | solution.py:117
  80.7 4.2 %collective-permute-start.4 = (f32[1,128]{1,0:T(1,128)S(1)}, f32[1,128]{1,0:T(1,128)S(1)}, u32[]{:S(2)}, u32[]{:S(2)}) collective-permute-start(f32[1,128]{1,0:T(1,128)S(1)} %add.84), channel_id=1, source_target_pairs={{0,2},{1,3},{2,0},{3,1},{4,6},{5,7},{6,4},{7,5},{8,10},{9,11},{10,... | collective-permute-start | bytes 1544 | tf_op jit(solution)/shard_map/ppermute | solution.py:117
  84.9 3.0 %collective-permute-start.5 = (f32[1,128]{1,0:T(1,128)S(1)}, f32[1,128]{1,0:T(1,128)S(1)}, u32[]{:S(2)}, u32[]{:S(2)}) collective-permute-start(f32[1,128]{1,0:T(1,128)S(1)} %add.85), channel_id=1, source_target_pairs={{0,4},{4,0},{8,12},{12,8},{16,20},{20,16},{24,28},{28,24},{32,36},... | collective-permute-start | bytes 1544 | tf_op jit(solution)/shard_map/ppermute | solution.py:117
  87.9 2.7 %collective-permute-start.6 = (f32[1,128]{1,0:T(1,128)S(1)}, f32[1,128]{1,0:T(1,128)S(1)}, u32[]{:S(2)}, u32[]{:S(2)}) collective-permute-start(f32[1,128]{1,0:T(1,128)S(1)} %add.86), channel_id=1, source_target_pairs={{0,8},{4,12},{8,0},{12,4},{16,24},{20,28},{24,16},{28,20},{32,40},... | collective-permute-start | bytes 1544 | tf_op jit(solution)/shard_map/ppermute | solution.py:117
  90.6 4.2 %collective-permute-start.7 = (f32[1,128]{1,0:T(1,128)S(1)}, f32[1,128]{1,0:T(1,128)S(1)}, u32[]{:S(2)}, u32[]{:S(2)}) collective-permute-start(f32[1,128]{1,0:T(1,128)S(1)} %add.87), channel_id=1, source_target_pairs={{0,16},{4,20},{8,24},{12,28},{16,0},{20,4},{24,8},{28,12},{32,48},... | collective-permute-start | bytes 1544 | tf_op jit(solution)/shard_map/ppermute | solution.py:117
  94.8 29.6 %collective-permute-start.8 = (f32[1,128]{1,0:T(1,128)S(1)}, f32[1,128]{1,0:T(1,128)S(1)}, u32[]{:S(2)}, u32[]{:S(2)}) collective-permute-start(f32[1,128]{1,0:T(1,128)S(1)} %add.88), channel_id=1, source_target_pairs={{0,32},{4,36},{8,40},{12,44},{16,48},{20,52},{24,56},{28,60},{32,0... | collective-permute-start | bytes 1544 | tf_op jit(solution)/shard_map/ppermute | solution.py:117
  124.4 3.6 %collective-permute-start.9 = (f32[1,128]{1,0:T(1,128)S(1)}, f32[1,128]{1,0:T(1,128)S(1)}, u32[]{:S(2)}, u32[]{:S(2)}) collective-permute-start(f32[1,128]{1,0:T(1,128)S(1)} %add.89), channel_id=1, source_target_pairs={{0,64},{4,68},{8,72},{12,76},{16,80},{20,84},{24,88},{28,92},{32,9... | collective-permute-start | bytes 1544 | tf_op jit(solution)/shard_map/ppermute | solution.py:117
  128.1 6.3 %collective-permute-start.10 = (f32[1,128]{1,0:T(1,128)S(1)}, f32[1,128]{1,0:T(1,128)S(1)}, u32[]{:S(2)}, u32[]{:S(2)}) collective-permute-start(f32[1,128]{1,0:T(1,128)S(1)} %add.90), channel_id=1, source_target_pairs={{0,128},{4,132},{8,136},{12,140},{16,144},{20,148},{24,152},{28,15... | collective-permute-start | bytes 1544 | tf_op jit(solution)/shard_map/ppermute | solution.py:117

commit v4 on v3

v4 whole, which is shorter than its diff:
```python
import functools

import jax
import jax.numpy as jnp
from jax import lax
from jax.experimental import pallas as pl
from jax.experimental.pallas import tpu as pltpu
from jax.sharding import PartitionSpec as P

THIRD = 64
MEMB = 128
WINDOW = 2
LEVELS = 64
LANES = 128
STEPS = 4
VMEM_LIMIT = 24 * 1024 * 1024


def blend(low, high, shift):
    sub = lax.broadcasted_iota(jnp.int32, low.shape, 0)
    return jnp.where(sub < shift, low, high)


def pack_kernel(x_ref, out_ref, x_buf, out_buf, in_sem, out_sem):
    steps, lines = out_buf.shape[0], out_buf.shape[1] // LEVELS
    blocks = lines // 2
    width = blocks * LANES
    n1 = lax.axis_index("pairs")
    tile, shift = n1 // 8, n1 % 8
    loads = [
        pltpu.make_async_copy(x_ref.at[:, :, pl.ds(k * width, width)], x_buf.at[k], in_sem.at[k])
        for k in range(steps)
    ]
    stores = [
        pltpu.make_async_copy(
            out_buf.at[k].reshape(LEVELS, lines, LANES), out_ref.at[:, pl.ds(k * lines, lines), :], out_sem.at[k]
        )
        for k in range(steps)
    ]
    for load in loads:
        load.start()
    for k in range(steps):
        loads[k].wait()
        for part in range(2):
            for j in range(blocks):
                lanes = slice(j * LANES, (j + 1) * LANES)
                turned = [
                    pltpu.roll(x_buf[k, part, 8 * a : 8 * a + 8, lanes], shift, 0) for a in range(LEVELS // 8)
                ]
                for a in range(LEVELS // 8):
                    slot = 8 * ((a + tile) % 8)
                    out_buf[k, pl.ds(slot * lines + part * blocks + j, 8, stride=lines), :] = blend(
                        turned[a - 1], turned[a], shift
                    )
        stores[k].start()
    for store in stores:
        store.wait()


def split(values):
    high = values.astype(jnp.bfloat16)
    return high, (values - high.astype(jnp.float32)).astype(jnp.bfloat16)


def mix_kernel(col_count, x_ref, pieces_ref, out_ref, moment_ref, out_buf, out_sem):
    steps, lines = out_buf.shape[0], out_buf.shape[1] // LEVELS
    blocks = lines // 2
    pitch = steps * lines
    source = x_ref.reshape(LEVELS * pitch, LANES)
    stores = [
        pltpu.make_async_copy(
            out_buf.at[k].reshape(LEVELS, lines, LANES), out_ref.at[:, pl.ds(k * lines, lines), :], out_sem.at[k]
        )
        for k in range(steps)
    ]
    owner = lax.axis_index("pairs")
    base = lax.axis_index("cols") * (col_count // (MEMB * WINDOW))
    row = lax.broadcasted_iota(jnp.int32, (LEVELS, LANES), 0)
    col = lax.broadcasted_iota(jnp.int32, (LEVELS, LANES), 1)
    low = pieces_ref[0]
    high = pltpu.roll(pltpu.roll(pieces_ref[1], owner + 1, 0), owner + 1, 1)
    zero = jnp.zeros_like(low)
    low = jnp.where((row <= owner) & (col <= owner), low, zero)
    high = jnp.where((row > owner) & (col > owner) & (col < LEVELS), high, zero)
    top, rest = split((low + high)[:, :LEVELS])
    matrix = jnp.concatenate([top, top, rest], 1)
    total = jnp.zeros((LEVELS, LANES), jnp.float32)
    for k in range(steps):
        for line in range(0, lines, 2):
            top, rest = split(
                jnp.concatenate([source[pl.ds(k * lines + line + i, LEVELS, stride=pitch), :] for i in range(2)], 1)
            )
            mixed = jnp.dot(matrix, jnp.concatenate([top, rest, top], 0), preferred_element_type=jnp.float32)
            for i in range(2):
                out = mixed[:, i * LANES : (i + 1) * LANES]
                out_buf[k, pl.ds(line + i, LEVELS, stride=lines), :] = out
                third = base + (k * blocks + (line + i) % blocks) * LANES // (MEMB * WINDOW)
                total += (third + 1).astype(jnp.float32) * (out * out)
        stores[k].start()
    moment_ref[...] = jnp.sum(total * (row + 1).astype(jnp.float32), axis=0, keepdims=True)
    for store in stores:
        store.wait()


def turn_kernel(x_ref, cos_tile_ref, sin_tile_ref, cos_row_ref, sin_row_ref, out_ref, out_buf, out_sem):
    steps, width = out_buf.shape[0], out_buf.shape[3]
    blocks = width // LANES
    lines = 2 * blocks
    pitch = steps * lines
    flat = x_ref.reshape(LEVELS * pitch, LANES)
    n1 = lax.axis_index("pairs")
    tile, shift = n1 // 8, n1 % 8
    back = (8 - shift) % 8
    stores = [
        pltpu.make_async_copy(out_buf.at[k], out_ref.at[:, :, pl.ds(k * width, width)], out_sem.at[k])
        for k in range(steps)
    ]

    def rows(line):
        turned = []
        for a in range(LEVELS // 8):
            slot = 8 * ((a + tile) % 8)
            turned.append(pltpu.roll(flat[pl.ds(slot * pitch + line, 8, stride=pitch), :], back, 0))
        return [blend(turned[a], turned[(a + 1) % 8], 8 - shift) for a in range(LEVELS // 8)]

    for k in range(steps):
        for j in range(blocks):
            lanes = slice(j * LANES, (j + 1) * LANES)
            wide = slice(k * width + j * LANES, k * width + (j + 1) * LANES)
            real, imag = rows(k * lines + j), rows(k * lines + blocks + j)
            cos_row, sin_row = cos_row_ref[:, wide], sin_row_ref[:, wide]
            for a in range(LEVELS // 8):
                span = slice(8 * a, 8 * a + 8)
                cos_tile = cos_tile_ref[a : a + 1, wide]
                sin_tile = sin_tile_ref[a : a + 1, wide]
                cosine = cos_tile * cos_row - sin_tile * sin_row
                sine = sin_tile * cos_row + cos_tile * sin_row
                out_buf[k, 0, span, lanes] = cosine * real[a] - sine * imag[a]
                out_buf[k, 1, span, lanes] = sine * real[a] + cosine * imag[a]
        stores[k].start()
    for store in stores:
        store.wait()


def butterfly(value, axis, last):
    size = lax.axis_size(axis)

    def partner(reach):
        return lax.ppermute(value, axis, [(i, i ^ reach) for i in range(size)])

    reach = 1
    while reach < size // last:
        value = value + partner(reach)
        reach *= 2
    terms = [value] + [partner(reach * i) for i in range(1, last)]
    while len(terms) > 1:
        terms = [terms[i] + terms[i + 1] for i in range(0, len(terms), 2)]
    return terms[0]


def local(state, sector_mix, kerr_rates, column_load):
    pair_count = lax.axis_size("pairs")
    col_devices = lax.axis_size("cols")
    device = lax.axis_index("pairs")
    col_device = lax.axis_index("cols")
    levels, col_count = state.shape[2], state.shape[3]
    assert pair_count == levels == LEVELS and state.shape[1] == 1
    state = state.reshape(2, levels, col_count)
    blocks = col_count // LANES
    lines = 2 * blocks
    part = blocks // STEPS
    width = part * LANES
    params = pltpu.CompilerParams(vmem_limit_bytes=VMEM_LIMIT)

    def exchange(rows):
        return lax.all_to_all(rows, "pairs", 0, 0, tiled=True)

    low = lax.dynamic_slice_in_dim(sector_mix, device, 1, 0)
    high = lax.dynamic_slice_in_dim(sector_mix, jnp.minimum(device + levels, 2 * levels - 2), 1, 0)
    mine = jnp.concatenate([low, high], 0)
    share = mine.shape[2]
    pieces = jnp.zeros((2, levels, LANES), jnp.float32)
    for step in range(col_devices):
        ring = [(i, (i + step) % col_devices) for i in range(col_devices)]
        received = lax.ppermute(mine, "cols", ring) if step else mine
        owner = (col_device - step) % col_devices
        pieces = lax.dynamic_update_slice(pieces, received, (0, 0, owner * share))

    anywhere = pl.BlockSpec(memory_space=pl.ANY)
    vmem = pl.BlockSpec(memory_space=pltpu.VMEM)
    rows_shape = pltpu.HBM((levels, lines, LANES), jnp.float32)
    rows_buf = pltpu.VMEM((STEPS, levels * 2 * part, LANES), jnp.float32)
    state_buf = pltpu.VMEM((STEPS, 2, levels, width), jnp.float32)
    sems = pltpu.SemaphoreType.DMA((STEPS,))

    packed = pl.pallas_call(
        pack_kernel,
        in_specs=[anywhere],
        out_specs=anywhere,
        out_shape=rows_shape,
        scratch_shapes=[state_buf, rows_buf, sems, sems],
        compiler_params=params,
        name="pack",
    )(pltpu.with_memory_space_constraint(state, pltpu.HBM))
    arrived = exchange(packed)

    n1 = device.astype(jnp.float32)
    eight = jnp.arange(8).astype(jnp.float32)
    loads = column_load.astype(jnp.float32)[None, :]
    tile_phases = (kerr_rates[0] * n1 + kerr_rates[1] * (8.0 * eight))[:, None] * loads
    row_phases = (kerr_rates[1] * eight)[:, None] * loads
    tables = (jnp.cos(tile_phases), jnp.sin(tile_phases), jnp.cos(row_phases), jnp.sin(row_phases))
    arrived, tables = lax.optimization_barrier((arrived, tables))

    mixed, moment = pl.pallas_call(
        functools.partial(mix_kernel, col_count),
        in_specs=[vmem, vmem],
        out_specs=[anywhere, vmem],
        out_shape=[rows_shape, jax.ShapeDtypeStruct((1, LANES), jnp.float32)],
        scratch_shapes=[rows_buf, sems],
        compiler_params=params,
        name="mix",
    )(arrived, pieces)
    returned = exchange(mixed)

    summed = jnp.sum(butterfly(butterfly(moment, "cols", 2), "pairs", 8))
    moment = summed / float(levels * levels * col_count * col_devices * levels * THIRD)

    evolved = pl.pallas_call(
        turn_kernel,
        in_specs=[vmem] * 5,
        out_specs=anywhere,
        out_shape=pltpu.HBM((2, levels, col_count), jnp.float32),
        scratch_shapes=[state_buf, sems],
        compiler_params=params,
        name="turn",
    )(returned, *tables)
    return evolved.reshape(2, 1, levels, col_count), moment.reshape(1)


def solution(mesh):
    placed = (P(None, "pairs", None, "cols"), P(None, None, "cols"), P(), P("cols"))
    return jax.shard_map(
        local,
        mesh=mesh,
        in_specs=placed,
        out_specs=(P(None, "pairs", None, "cols"), P()),
        check_vma=False,
    )
```

time: 143 us -> 136 us (0.951)
  starting transfers between devices: 41.4 us -> 49.5 us
  waiting for transfers between devices: 73.1 us -> 65.7 us
  other arithmetic: 6.14 us -> 2.25 us
  Pallas kernels: 11.4 us -> 7.9 us
    ppermute x8 -> x12, waiting for transfers between devices: 40.2 us -> 29.5 us  [partner(): return lax.ppermute(value, axis, [(i, i ^ reach) for i in range(size)])]
    ppermute x8 -> x12, starting transfers between devices: 16.3 us -> 24.4 us  [partner(): return lax.ppermute(value, axis, [(i, i ^ reach) for i in range(size)])]
    sin x1, other arithmetic: 4.81 us -> 0.99 us  [local(): jnp.sin(row_phases)]
    pallas_call x3, Pallas kernels: 11.4 us -> 7.9 us  [the longest x1 2.96 us: local(): pl.pallas_call(pack_kernel, in_specs=[anywhere], out_specs=anywhere, out_...]
    all_to_all x2, waiting for transfers between devices: 33 us -> 36.2 us  [exchange(): return lax.all_to_all(rows, 'pairs', 0, 0, tiled=True)]
  transfers between devices with their start and end apart: 13 -> 17, of which waited for: 9 -> 9; matrix products, arithmetic and copies ran while one was open for 8% -> 6% of each run, Pallas kernels for 0% -> 0%
where the time goes in v4:
time: 136 us; the launch traced here: 135 us
  waiting for transfers between devices  65.7 us (48%)
  starting transfers between devices  49.5 us (36%)
  Pallas kernels  7.9 us (6%)
  local copies, waits for them, and re-layouts  5.58 us (4%)
  between operations  3.98 us (3%)
  other arithmetic  2.25 us (2%)
    all_to_all x2, waiting for transfers between devices, exchange(): return lax.all_to_all(rows, 'pairs', 0, 0, tiled=True)  36.2 us
    ppermute x12, waiting for transfers between devices, partner(): return lax.ppermute(value, axis, [(i, i ^ reach) for i in range(size)])  29.5 us
    ppermute x12, starting transfers between devices, partner(): return lax.ppermute(value, axis, [(i, i ^ reach) for i in range(size)])  24.4 us
    all_to_all x2, starting transfers between devices, exchange(): return lax.all_to_all(rows, 'pairs', 0, 0, tiled=True)  20.3 us
    ppermute x3, starting transfers between devices, local(): received = lax.ppermute(mine, 'cols', ring) if step else mine  4.85 us
    pallas_call x1, Pallas kernels, local(): pl.pallas_call(pack_kernel, in_specs=[anywhere], out_specs=anywhere, out_...  2.96 us
    pallas_call x1, Pallas kernels, local(): pl.pallas_call(functools.partial(mix_kernel, col_count), in_specs=[vmem,...  2.83 us
  transfers between devices with their start and end apart: 17, of which 9 were waited for; matrix products, arithmetic and copies ran while one was open for 6% of the time, Pallas kernels for 0%

profile of v4, /device:TPU:1, one launch (start us, length us, event | category | flops | bytes accessed | tf_op | source)
XLA Modules:
  0.0 134.9 jit_solution(8010394984583352723)
XLA Ops:
  0.6 3.0 %pack.1 = f32[64,64,128]{2,1,0:T(8,128)} custom-call(f32[2,64,4096]{2,1,0:T(8,128)} %bitcast.7), custom_call_target="tpu_custom_call" | custom-call | tf_op jit(solution)/shard_map/pack/pallas_call | solution.py:196
  3.6 0.0 copy-start
  3.6 13.3 %all-to-all-start = ((f32[64,64,128]{2,1,0:T(8,128)}), f32[64,64,128]{2,1,0:T(8,128)S(1)}, u32[]{:S(2)}, u32[]{:S(2)}) async-start(f32[64,64,128]{2,1,0:T(8,128)} %pack.1), calls=%async_computation | async-start | bytes 4194304 | tf_op jit(solution)/shard_map/all_to_all | solution.py:176
  16.9 0.0 copy-start.1
  16.9 0.0 copy-start.2
  16.9 1.1 constant_dynamic-slice_fusion.1
  18.1 1.3 copy.17
  19.4 0.3 copy.16
  19.6 0.1 copy.11
  19.7 1.2 collective-permute-start
  21.0 2.5 %collective-permute-start.1 = (f32[2,64,16]{2,1,0:T(8,128)S(1)}, f32[2,64,16]{2,1,0:T(8,128)S(1)}, u32[]{:S(2)}, u32[]{:S(2)}) collective-permute-start(f32[2,64,16]{2,1,0:T(8,128)S(1)} %copy.11), channel_id=1, source_target_pairs={{0,2},{1,3},{2,0},{3,1},{4,6},{5,7},{6,4},{7,5},{8,10},{9,11},{10,... | collective-permute-start | bytes 24584 | tf_op jit(solution)/shard_map/ppermute | solution.py:185
  23.4 1.2 collective-permute-start.2
  24.6 0.6 fusion
  26.5 0.6 multiply_add_fusion
  27.1 1.0 multiply_sine_fusion
  28.2 0.3 dynamic_update_slice.12
  28.5 0.0 collective-permute-done
  28.5 0.6 dynamic_update_slice.13
  29.2 0.0 collective-permute-done.1
  29.2 0.6 dynamic_update_slice.14
  29.8 0.6 dynamic_update_slice.15.pieces_ref
  30.4 36.2 %all-to-all-done.x_ref = f32[64,64,128]{2,1,0:T(8,128)S(1)} async-done(((f32[64,64,128]{2,1,0:T(8,128)}), f32[64,64,128]{2,1,0:T(8,128)S(1)}, u32[]{:S(2)}, u32[]{:S(2)}) %all-to-all-start) | async-done | bytes 2097184 | tf_op jit(solution)/shard_map/all_to_all | solution.py:176
  66.6 2.8 %mix.1 = (f32[64,64,128]{2,1,0:T(8,128)}, f32[1,128]{1,0:T(1,128)S(1)}) custom-call(f32[64,64,128]{2,1,0:T(8,128)S(1)} %all-to-all-done.x_ref, f32[2,64,128]{2,1,0:T(8,128)S(1)} %dynamic_update_slice.15.pieces_ref), custom_call_target="tpu_custom_call" | custom-call | tf_op jit(solution)/shard_map/mix/pallas_call | solution.py:215
  69.4 7.0 %all-to-all-start.1 = ((f32[64,64,128]{2,1,0:T(8,128)}), f32[64,64,128]{2,1,0:T(8,128)S(1)}, u32[]{:S(2)}, u32[]{:S(2)}) async-start(f32[64,64,128]{2,1,0:T(8,128)} %get-tuple-element.10), calls=%async_computation.1 | async-start | bytes 4194304 | tf_op jit(solution)/shard_map/all_to_all | solution.py:176
  76.4 1.3 collective-permute-start.3
  77.7 1.5 %collective-permute-done.3 = f32[1,128]{1,0:T(1,128)S(1)} collective-permute-done((f32[1,128]{1,0:T(1,128)S(1)}, f32[1,128]{1,0:T(1,128)S(1)}, u32[]{:S(2)}, u32[]{:S(2)}) %collective-permute-start.3) | collective-permute-done | bytes 544 | tf_op jit(solution)/shard_map/ppermute | solution.py:149
  79.2 2.7 %collective-permute-start.4 = (f32[1,128]{1,0:T(1,128)S(1)}, f32[1,128]{1,0:T(1,128)S(1)}, u32[]{:S(2)}, u32[]{:S(2)}) collective-permute-start(f32[1,128]{1,0:T(1,128)S(1)} %add.96), channel_id=1, source_target_pairs={{0,2},{1,3},{2,0},{3,1},{4,6},{5,7},{6,4},{7,5},{8,10},{9,11},{10,... | collective-permute-start | bytes 1544 | tf_op jit(solution)/shard_map/ppermute | solution.py:149
  82.0 1.5 %collective-permute-done.4 = f32[1,128]{1,0:T(1,128)S(1)} collective-permute-done((f32[1,128]{1,0:T(1,128)S(1)}, f32[1,128]{1,0:T(1,128)S(1)}, u32[]{:S(2)}, u32[]{:S(2)}) %collective-permute-start.4) | collective-permute-done | bytes 544 | tf_op jit(solution)/shard_map/ppermute | solution.py:149
  83.5 2.2 %collective-permute-start.5 = (f32[1,128]{1,0:T(1,128)S(1)}, f32[1,128]{1,0:T(1,128)S(1)}, u32[]{:S(2)}, u32[]{:S(2)}) collective-permute-start(f32[1,128]{1,0:T(1,128)S(1)} %add.97), channel_id=1, source_target_pairs={{0,4},{4,0},{8,12},{12,8},{16,20},{20,16},{24,28},{28,24},{32,36},... | collective-permute-start | bytes 1544 | tf_op jit(solution)/shard_map/ppermute | solution.py:149
  85.6 0.8 collective-permute-done.5
  86.4 1.3 collective-permute-start.6
  87.7 1.4 %collective-permute-done.6 = f32[1,128]{1,0:T(1,128)S(1)} collective-permute-done((f32[1,128]{1,0:T(1,128)S(1)}, f32[1,128]{1,0:T(1,128)S(1)}, u32[]{:S(2)}, u32[]{:S(2)}) %collective-permute-start.6) | collective-permute-done | bytes 544 | tf_op jit(solution)/shard_map/ppermute | solution.py:149
  89.2 2.9 %collective-permute-start.7 = (f32[1,128]{1,0:T(1,128)S(1)}, f32[1,128]{1,0:T(1,128)S(1)}, u32[]{:S(2)}, u32[]{:S(2)}) collective-permute-start(f32[1,128]{1,0:T(1,128)S(1)} %add.99), channel_id=1, source_target_pairs={{0,16},{4,20},{8,24},{12,28},{16,0},{20,4},{24,8},{28,12},{32,48},... | collective-permute-start | bytes 1544 | tf_op jit(solution)/shard_map/ppermute | solution.py:149
  92.0 1.4 %collective-permute-done.7 = f32[1,128]{1,0:T(1,128)S(1)} collective-permute-done((f32[1,128]{1,0:T(1,128)S(1)}, f32[1,128]{1,0:T(1,128)S(1)}, u32[]{:S(2)}, u32[]{:S(2)}) %collective-permute-start.7) | collective-permute-done | bytes 544 | tf_op jit(solution)/shard_map/ppermute | solution.py:149
  93.4 3.3 %collective-permute-start.13 = (f32[1,128]{1,0:T(1,128)S(1)}, f32[1,128]{1,0:T(1,128)S(1)}, u32[]{:S(2)}, u32[]{:S(2)}) collective-permute-start(f32[1,128]{1,0:T(1,128)S(1)} %add.100), channel_id=1, source_target_pairs={{0,192},{4,196},{8,200},{12,204},{16,208},{20,212},{24,216},{28,22... | collective-permute-start | bytes 1544 | tf_op jit(solution)/shard_map/ppermute | solution.py:149
  96.7 0.4 collective-permute-start.14
  97.1 4.3 %collective-permute-start.11 = (f32[1,128]{1,0:T(1,128)S(1)}, f32[1,128]{1,0:T(1,128)S(1)}, u32[]{:S(2)}, u32[]{:S(2)}) collective-permute-start(f32[1,128]{1,0:T(1,128)S(1)} %add.100), channel_id=1, source_target_pairs={{0,128},{4,132},{8,136},{12,140},{16,144},{20,148},{24,152},{28,15... | collective-permute-start | bytes 1544 | tf_op jit(solution)/shard_map/ppermute | solution.py:149
  101.4 0.9 collective-permute-start.12
  102.3 1.3 collective-permute-start.9
  103.6 20.6 %collective-permute-done.13 = f32[1,128]{1,0:T(1,128)S(1)} collective-permute-done((f32[1,128]{1,0:T(1,128)S(1)}, f32[1,128]{1,0:T(1,128)S(1)}, u32[]{:S(2)}, u32[]{:S(2)}) %collective-permute-start.13) | collective-permute-done | bytes 544 | tf_op jit(solution)/shard_map/ppermute | solution.py:149
  124.2 3.8 %collective-permute-start.10 = (f32[1,128]{1,0:T(1,128)S(1)}, f32[1,128]{1,0:T(1,128)S(1)}, u32[]{:S(2)}, u32[]{:S(2)}) collective-permute-start(f32[1,128]{1,0:T(1,128)S(1)} %add.100), channel_id=1, source_target_pairs={{0,96},{4,100},{8,104},{12,108},{16,112},{20,116},{24,120},{28,124... | collective-permute-start | bytes 1544 | tf_op jit(solution)/shard_map/ppermute | solution.py:149
  128.0 0.0 collective-permute-done.14
  128.0 0.0 collective-permute-start.8
  128.0 0.0 collective-permute-done.12
  128.0 0.9 collective-permute-done.10
  129.0 1.5 %collective-permute-done.8 = f32[1,128]{1,0:T(1,128)S(1)} collective-permute-done((f32[1,128]{1,0:T(1,128)S(1)}, f32[1,128]{1,0:T(1,128)S(1)}, u32[]{:S(2)}, u32[]{:S(2)}) %collective-permute-start.8) | collective-permute-done | bytes 544 | tf_op jit(solution)/shard_map/ppermute | solution.py:149
  130.4 0.6 add_reduce_fusion
  131.7 2.1 %turn.1 = f32[2,64,4096]{2,1,0:T(8,128)} custom-call(f32[64,64,128]{2,1,0:T(8,128)S(1)} %all-to-all-done.1.x_ref, f32[8,4096]{1,0:T(8,128)S(1)} %get-tuple-element.11.cos_tile_ref, f32[8,4096]{1,0:T(8,128)S(1)} %get-tuple-element.12.sin_tile_ref, f32[8,4096]{1,0:T(8,128)S(1)} %get-tuple-element.13.cos_row_ref, f32[8,4096]{1,0:T(8,128)S(1)} %get-tuple-element.14.sin_row_ref), custom_call_target="tpu_custom_call" | custom-call | tf_op jit(solution)/shard_map/turn/pallas_call | solution.py:229
  (15 shorter events, 0.0 us)
Async XLA Ops:
  3.6 13.3 %copy-start = (f32[127,64,16]{0,2,1:T(8,128)S(1)}, f32[127,64,16]{0,2,1:T(8,128)}, u32[]{:S(2)}) copy-start(f32[127,64,16]{0,2,1:T(8,128)} %param.5) | copy-start | bytes 1560580
  3.6 63.0 %all-to-all-start = ((f32[64,64,128]{2,1,0:T(8,128)}), f32[64,64,128]{2,1,0:T(8,128)S(1)}, u32[]{:S(2)}, u32[]{:S(2)}) async-start(f32[64,64,128]{2,1,0:T(8,128)} %pack.1), calls=%async_computation | async-start | bytes 4194304 | tf_op jit(solution)/shard_map/all_to_all | solution.py:176
  16.9 7.7 %copy-start.1 = (s32[4096]{0:T(1024)S(1)}, s32[4096]{0:T(1024)}, u32[]{:S(2)}) copy-start(s32[4096]{0:T(1024)} %param.7) | copy-start | bytes 49156
  16.9 7.7 %copy-start.2 = (f32[2]{0:T(128)S(1)}, f32[2]{0:T(128)}, u32[]{:S(2)}) copy-start(f32[2]{0:T(128)} %param.6) | copy-start | bytes 28
  19.7 8.8 %collective-permute-start = (f32[2,64,16]{2,1,0:T(8,128)S(1)}, f32[2,64,16]{2,1,0:T(8,128)S(1)}, u32[]{:S(2)}, u32[]{:S(2)}) collective-permute-start(f32[2,64,16]{2,1,0:T(8,128)S(1)} %copy.11), channel_id=1, source_target_pairs={{0,1},{1,2},{2,3},{3,0},{4,5},{5,6},{6,7},{7,4},{8,9},{9,10},{10,1... | collective-permute-start | bytes 24584 | tf_op jit(solution)/shard_map/ppermute | solution.py:185
  21.0 8.2 %collective-permute-start.1 = (f32[2,64,16]{2,1,0:T(8,128)S(1)}, f32[2,64,16]{2,1,0:T(8,128)S(1)}, u32[]{:S(2)}, u32[]{:S(2)}) collective-permute-start(f32[2,64,16]{2,1,0:T(8,128)S(1)} %copy.11), channel_id=1, source_target_pairs={{0,2},{1,3},{2,0},{3,1},{4,6},{5,7},{6,4},{7,5},{8,10},{9,11},{10,... | collective-permute-start | bytes 24584 | tf_op jit(solution)/shard_map/ppermute | solution.py:185
  23.4 6.4 %collective-permute-start.2 = (f32[2,64,16]{2,1,0:T(8,128)S(1)}, f32[2,64,16]{2,1,0:T(8,128)S(1)}, u32[]{:S(2)}, u32[]{:S(2)}) collective-permute-start(f32[2,64,16]{2,1,0:T(8,128)S(1)} %copy.11), channel_id=1, source_target_pairs={{0,3},{1,0},{2,1},{3,2},{4,7},{5,4},{6,5},{7,6},{8,11},{9,8},{10,9... | collective-permute-start | bytes 24584 | tf_op jit(solution)/shard_map/ppermute | solution.py:185
  69.4 62.2 %all-to-all-start.1 = ((f32[64,64,128]{2,1,0:T(8,128)}), f32[64,64,128]{2,1,0:T(8,128)S(1)}, u32[]{:S(2)}, u32[]{:S(2)}) async-start(f32[64,64,128]{2,1,0:T(8,128)} %get-tuple-element.10), calls=%async_computation.1 | async-start | bytes 4194304 | tf_op jit(solution)/shard_map/all_to_all | solution.py:176
  76.4 2.8 %collective-permute-start.3 = (f32[1,128]{1,0:T(1,128)S(1)}, f32[1,128]{1,0:T(1,128)S(1)}, u32[]{:S(2)}, u32[]{:S(2)}) collective-permute-start(f32[1,128]{1,0:T(1,128)S(1)} %get-tuple-element.15), channel_id=1, source_target_pairs={{0,1},{1,0},{2,3},{3,2},{4,5},{5,4},{6,7},{7,6},{8,9},{9,8},{10,11... | collective-permute-start | bytes 1544 | tf_op jit(solution)/shard_map/ppermute | solution.py:149
  79.2 4.2 %collective-permute-start.4 = (f32[1,128]{1,0:T(1,128)S(1)}, f32[1,128]{1,0:T(1,128)S(1)}, u32[]{:S(2)}, u32[]{:S(2)}) collective-permute-start(f32[1,128]{1,0:T(1,128)S(1)} %add.96), channel_id=1, source_target_pairs={{0,2},{1,3},{2,0},{3,1},{4,6},{5,7},{6,4},{7,5},{8,10},{9,11},{10,... | collective-permute-start | bytes 1544 | tf_op jit(solution)/shard_map/ppermute | solution.py:149
  83.5 3.0 %collective-permute-start.5 = (f32[1,128]{1,0:T(1,128)S(1)}, f32[1,128]{1,0:T(1,128)S(1)}, u32[]{:S(2)}, u32[]{:S(2)}) collective-permute-start(f32[1,128]{1,0:T(1,128)S(1)} %add.97), channel_id=1, source_target_pairs={{0,4},{4,0},{8,12},{12,8},{16,20},{20,16},{24,28},{28,24},{32,36},... | collective-permute-start | bytes 1544 | tf_op jit(solution)/shard_map/ppermute | solution.py:149
  86.4 2.7 %collective-permute-start.6 = (f32[1,128]{1,0:T(1,128)S(1)}, f32[1,128]{1,0:T(1,128)S(1)}, u32[]{:S(2)}, u32[]{:S(2)}) collective-permute-start(f32[1,128]{1,0:T(1,128)S(1)} %add.98), channel_id=1, source_target_pairs={{0,8},{4,12},{8,0},{12,4},{16,24},{20,28},{24,16},{28,20},{32,40},... | collective-permute-start | bytes 1544 | tf_op jit(solution)/shard_map/ppermute | solution.py:149
  89.2 4.2 %collective-permute-start.7 = (f32[1,128]{1,0:T(1,128)S(1)}, f32[1,128]{1,0:T(1,128)S(1)}, u32[]{:S(2)}, u32[]{:S(2)}) collective-permute-start(f32[1,128]{1,0:T(1,128)S(1)} %add.99), channel_id=1, source_target_pairs={{0,16},{4,20},{8,24},{12,28},{16,0},{20,4},{24,8},{28,12},{32,48},... | collective-permute-start | bytes 1544 | tf_op jit(solution)/shard_map/ppermute | solution.py:149
  93.4 30.8 %collective-permute-start.13 = (f32[1,128]{1,0:T(1,128)S(1)}, f32[1,128]{1,0:T(1,128)S(1)}, u32[]{:S(2)}, u32[]{:S(2)}) collective-permute-start(f32[1,128]{1,0:T(1,128)S(1)} %add.100), channel_id=1, source_target_pairs={{0,192},{4,196},{8,200},{12,204},{16,208},{20,212},{24,216},{28,22... | collective-permute-start | bytes 1544 | tf_op jit(solution)/shard_map/ppermute | solution.py:149
  96.7 31.3 %collective-permute-start.14 = (f32[1,128]{1,0:T(1,128)S(1)}, f32[1,128]{1,0:T(1,128)S(1)}, u32[]{:S(2)}, u32[]{:S(2)}) collective-permute-start(f32[1,128]{1,0:T(1,128)S(1)} %add.100), channel_id=1, source_target_pairs={{0,224},{4,228},{8,232},{12,236},{16,240},{20,244},{24,248},{28,25... | collective-permute-start | bytes 1544 | tf_op jit(solution)/shard_map/ppermute | solution.py:149
  97.1 30.9 %collective-permute-start.11 = (f32[1,128]{1,0:T(1,128)S(1)}, f32[1,128]{1,0:T(1,128)S(1)}, u32[]{:S(2)}, u32[]{:S(2)}) collective-permute-start(f32[1,128]{1,0:T(1,128)S(1)} %add.100), channel_id=1, source_target_pairs={{0,128},{4,132},{8,136},{12,140},{16,144},{20,148},{24,152},{28,15... | collective-permute-start | bytes 1544 | tf_op jit(solution)/shard_map/ppermute | solution.py:149
  101.4 26.6 %collective-permute-start.12 = (f32[1,128]{1,0:T(1,128)S(1)}, f32[1,128]{1,0:T(1,128)S(1)}, u32[]{:S(2)}, u32[]{:S(2)}) collective-permute-start(f32[1,128]{1,0:T(1,128)S(1)} %add.100), channel_id=1, source_target_pairs={{0,160},{4,164},{8,168},{12,172},{16,176},{20,180},{24,184},{28,18... | collective-permute-start | bytes 1544 | tf_op jit(solution)/shard_map/ppermute | solution.py:149
  102.3 25.7 %collective-permute-start.9 = (f32[1,128]{1,0:T(1,128)S(1)}, f32[1,128]{1,0:T(1,128)S(1)}, u32[]{:S(2)}, u32[]{:S(2)}) collective-permute-start(f32[1,128]{1,0:T(1,128)S(1)} %add.100), channel_id=1, source_target_pairs={{0,64},{4,68},{8,72},{12,76},{16,80},{20,84},{24,88},{28,92},{32,9... | collective-permute-start | bytes 1544 | tf_op jit(solution)/shard_map/ppermute | solution.py:149
  124.2 4.8 %collective-permute-start.10 = (f32[1,128]{1,0:T(1,128)S(1)}, f32[1,128]{1,0:T(1,128)S(1)}, u32[]{:S(2)}, u32[]{:S(2)}) collective-permute-start(f32[1,128]{1,0:T(1,128)S(1)} %add.100), channel_id=1, source_target_pairs={{0,96},{4,100},{8,104},{12,108},{16,112},{20,116},{24,120},{28,124... | collective-permute-start | bytes 1544 | tf_op jit(solution)/shard_map/ppermute | solution.py:149
  128.0 2.4 %collective-permute-start.8 = (f32[1,128]{1,0:T(1,128)S(1)}, f32[1,128]{1,0:T(1,128)S(1)}, u32[]{:S(2)}, u32[]{:S(2)}) collective-permute-start(f32[1,128]{1,0:T(1,128)S(1)} %add.100), channel_id=1, source_target_pairs={{0,32},{4,36},{8,40},{12,44},{16,48},{20,52},{24,56},{28,60},{32,0... | collective-permute-start | bytes 1544 | tf_op jit(solution)/shard_map/ppermute | solution.py:149
